TPU v7x, 128 devices: a whole 4x4x4 slice. The times are simulated.
128 devices in a mesh: row: 8 (over y, x_hi), col: 16 (over z, x_lo, core).
Axes of the slice: x: 4 (x_hi: 2, x_lo: 2; x = x_hi * 2 + x_lo), y: 4, z: 4, core: 2. Of those that a mesh axis runs over, the one named last changes fastest.
Arguments:
- front: float32 [16384, 16384], P('row', 'col'), may hold values from -6 to 6
- pivot: float32 [1024, 1024], P(('row', 'col')), as said below
- panel: float32 [16384, 1024], P(('row', 'col')), may hold values from -4 to 4
- child_blocks: bfloat16 [16384, 128, 128], P(('row', 'col')), may hold values from -6 to 6
- child_dest: int32 [16384, 1], P(('row', 'col')), may hold values from 0 to 127; in each aligned block of 128 rows (0 to 127, 128 to 255, ...) at most 2 rows name the same one
- child_pos: int32 [16384], P(('row', 'col')), may hold values from 0 to 127
- pattern: int32 [128, 128], P('row', 'col'), may hold values 0 or 1
Outputs:
- schur: float32 [16384, 16384], P('row', 'col')
- factor: float32 [16384, 1024], P(('row', 'col'))
Inputs may be any that keep to these rules, and one draw needn't show every extreme that they name: pivot is symmetric positive definite. `child_dest`: among the child blocks of one device no owner is named more than 2 times, a bound that some block reaches.
All inputs are finite; a program needn't handle non-finite values. No bound on the sum of `pattern` on one device may be relied on, other than what follows from the above.
Results may differ from a plain program's by a relative error of at most 0.0023.
Values may be sent and summed in bfloat16 or wider, within the bound.
A program may use at most 192 MiB of HBM per device.

v0:
```python
import jax
import jax.numpy as jnp
from jax import lax
from jax.sharding import PartitionSpec as P


def broadcast(block, axis, holder):
    block = jnp.where(lax.axis_index(axis) == holder, block, jnp.zeros_like(block))
    return lax.psum(block, axis)


def per_device(front, pivot, panel, child_blocks, child_dest, child_pos, pattern):
    rows_count = lax.axis_size("row")
    cols_count = lax.axis_size("col")
    devices = rows_count * cols_count
    tile_rows, tile_cols = front.shape
    side = child_blocks.shape[1]
    block_rows = tile_rows // side
    block_cols = tile_cols // side
    tile_count = block_rows * block_cols
    capacity = max(2, 2 * child_blocks.shape[0] // devices)
    owner = child_dest[:, 0]
    onehot = (owner[:, None] == jnp.arange(devices, dtype=jnp.int32)[None, :]).astype(jnp.int32)
    slot_index = jnp.sum(jnp.cumsum(onehot, axis=0) * onehot, axis=1) - 1
    target = owner * capacity + slot_index
    outgoing = (
        jnp.zeros((devices * capacity, side, side), jnp.bfloat16).at[target].set(child_blocks)
    )
    places = jnp.full((devices * capacity,), tile_count, jnp.int32).at[target].set(child_pos)
    arrived, spots = (
        lax.all_to_all(outgoing, ("row", "col"), split_axis=0, concat_axis=0, tiled=True),
        lax.all_to_all(places, ("row", "col"), split_axis=0, concat_axis=0, tiled=True),
    )
    pivot_whole = lax.all_gather(pivot, ("row", "col"), axis=0, tiled=True)
    lower_factor = jnp.linalg.cholesky(pivot_whole)
    own_rows = lax.linalg.triangular_solve(
        lower_factor, panel, left_side=False, lower=True, transpose_a=True
    )
    rounded = own_rows.astype(jnp.bfloat16)
    row_side = lax.all_gather(rounded, "col", axis=0, tiled=True)
    col_index = lax.axis_index("col")
    holder = col_index * tile_cols // tile_rows
    offset = col_index * tile_cols % tile_rows
    own_slice = lax.dynamic_slice_in_dim(row_side, offset, tile_cols, 0)
    col_side = broadcast(own_slice, "row", holder)
    tiles = (
        front.reshape(block_rows, side, block_cols, side)
        .transpose(0, 2, 1, 3)
        .reshape(tile_count, side, side)
    )
    tiles = tiles.at[spots].add(arrived.astype(jnp.float32), mode="drop")
    assembled = (
        tiles.reshape(block_rows, block_cols, side, side)
        .transpose(0, 2, 1, 3)
        .reshape(tile_rows, tile_cols)
    )
    update = jnp.dot(row_side, col_side.T, preferred_element_type=jnp.float32)
    masked = (
        update.reshape(block_rows, side, block_cols, side)
        * pattern.astype(jnp.float32)[:, None, :, None]
    )
    schur = assembled - masked.reshape(tile_rows, tile_cols)
    return (schur, own_rows)


def solution(mesh):
    return jax.shard_map(
        per_device,
        mesh=mesh,
        in_specs=(
            P("row", "col"),
            P(("row", "col"), None),
            P(("row", "col"), None),
            P(("row", "col"), None, None),
            P(("row", "col"), None),
            P(("row", "col")),
            P("row", "col"),
        ),
        out_specs=(P("row", "col"), P(("row", "col"), None)),
        check_vma=False,
    )
```

profile of v0, /device:TPU:92, one launch (start us, length us, event | category | flops | bytes accessed | tf_op | source)
XLA Modules:
  0.0 858.2 jit_solution(4850716802621796433)
XLA Ops:
  8.0 197.6 %all-gather.3.cloned.1.call-done = f32[1024,1024]{1,0:T(8,128)} async-done(((f32[8,1024]{1,0:T(8,128)}), f32[1024,1024]{1,0:T(8,128)}) %all-gather.3.cloned.1.call-update) | async-done | bytes 4194320 | tf_op jit(solution)/shard_map/all_gather | solution.py:34
  205.6 5.3 copy.27
  210.9 4.4 fusion.1
  217.3 11.7 %cholesky.223 = f32[128,128]{1,0:T(8,128)S(1)} custom-call(f32[128,128]{1,0:T(8,128)S(1)} %cholesky.580), custom_call_target="Cholesky" | custom-call | tf_op jit(solution)/shard_map/jit(cholesky)/cholesky | solution.py:35
  229.1 9.8 %custom-call.62 = f32[1,128,128]{1,2,0:T(8,128)S(1)} custom-call(f32[1,128,128]{2,1,0:T(8,128)S(1)} %get-tuple-element.74), custom_call_target="InvertDiagBlocksLowerTriangular" | custom-call | tf_op jit(solution)/shard_map/jit(cholesky)/cholesky | solution.py:35
  245.3 12.0 %cholesky.244 = f32[128,128]{1,0:T(8,128)S(1)} custom-call(f32[128,128]{1,0:T(8,128)S(1)} %cholesky.584), custom_call_target="Cholesky" | custom-call | tf_op jit(solution)/shard_map/jit(cholesky)/cholesky | solution.py:35
  258.0 9.8 %custom-call.63 = f32[1,128,128]{1,2,0:T(8,128)S(1)} custom-call(f32[1,128,128]{2,1,0:T(8,128)S(1)} %get-tuple-element.71), custom_call_target="InvertDiagBlocksLowerTriangular" | custom-call | tf_op jit(solution)/shard_map/jit(cholesky)/cholesky | solution.py:35
  271.1 11.7 %cholesky.468 = f32[128,128]{1,0:T(8,128)S(1)} custom-call(f32[128,128]{1,0:T(8,128)S(1)} %cholesky.589), custom_call_target="Cholesky" | custom-call | tf_op jit(solution)/shard_map/jit(cholesky)/cholesky | solution.py:35
  284.1 9.8 %custom-call.64 = f32[1,128,128]{1,2,0:T(8,128)S(1)} custom-call(f32[1,128,128]{2,1,0:T(8,128)S(1)} %get-tuple-element.68), custom_call_target="InvertDiagBlocksLowerTriangular" | custom-call | tf_op jit(solution)/shard_map/jit(cholesky)/cholesky | solution.py:35
  297.4 11.8 %cholesky.487 = f32[128,128]{1,0:T(8,128)S(1)} custom-call(f32[128,128]{1,0:T(8,128)S(1)} %cholesky.594), custom_call_target="Cholesky" | custom-call | tf_op jit(solution)/shard_map/jit(cholesky)/cholesky | solution.py:35
  310.6 9.8 %custom-call.65 = f32[1,128,128]{1,2,0:T(8,128)S(1)} custom-call(f32[1,128,128]{2,1,0:T(8,128)S(1)} %get-tuple-element.65), custom_call_target="InvertDiagBlocksLowerTriangular" | custom-call | tf_op jit(solution)/shard_map/jit(cholesky)/cholesky | solution.py:35
  323.8 11.7 %cholesky.506 = f32[128,128]{1,0:T(8,128)S(1)} custom-call(f32[128,128]{1,0:T(8,128)S(1)} %cholesky.599), custom_call_target="Cholesky" | custom-call | tf_op jit(solution)/shard_map/jit(cholesky)/cholesky | solution.py:35
  336.9 10.0 %custom-call.66 = f32[1,128,128]{1,2,0:T(8,128)S(1)} custom-call(f32[1,128,128]{2,1,0:T(8,128)S(1)} %get-tuple-element.62), custom_call_target="InvertDiagBlocksLowerTriangular" | custom-call | tf_op jit(solution)/shard_map/jit(cholesky)/cholesky | solution.py:35
  350.2 11.7 %cholesky.526 = f32[128,128]{1,0:T(8,128)S(1)} custom-call(f32[128,128]{1,0:T(8,128)S(1)} %cholesky.604), custom_call_target="Cholesky" | custom-call | tf_op jit(solution)/shard_map/jit(cholesky)/cholesky | solution.py:35
  363.2 9.8 %custom-call.67 = f32[1,128,128]{1,2,0:T(8,128)S(1)} custom-call(f32[1,128,128]{2,1,0:T(8,128)S(1)} %get-tuple-element.59), custom_call_target="InvertDiagBlocksLowerTriangular" | custom-call | tf_op jit(solution)/shard_map/jit(cholesky)/cholesky | solution.py:35
  376.1 12.1 %cholesky.546 = f32[128,128]{1,0:T(8,128)S(1)} custom-call(f32[128,128]{1,0:T(8,128)S(1)} %cholesky.609), custom_call_target="Cholesky" | custom-call | tf_op jit(solution)/shard_map/jit(cholesky)/cholesky | solution.py:35
  389.4 9.8 %custom-call.68 = f32[1,128,128]{1,2,0:T(8,128)S(1)} custom-call(f32[1,128,128]{2,1,0:T(8,128)S(1)} %get-tuple-element.56), custom_call_target="InvertDiagBlocksLowerTriangular" | custom-call | tf_op jit(solution)/shard_map/jit(cholesky)/cholesky | solution.py:35
  401.9 11.7 %cholesky.564 = f32[128,128]{1,0:T(8,128)S(1)} custom-call(f32[128,128]{1,0:T(8,128)S(1)} %convolution_subtract_fusion.11), custom_call_target="Cholesky" | custom-call | tf_op jit(solution)/shard_map/jit(cholesky)/cholesky | solution.py:35
  420.6 4.9 select_select_fusion
  425.5 23.5 %while.1 = (s32[]{:T(128)}, f32[1024,1024]{1,0:T(8,128)}, s32[8,2]{0,1:T(2,128)S(1)}, f32[8,128,128]{2,1,0:T(8,128)S(1)}, s32[]{:T(128)}) while((s32[]{:T(128)}, f32[1024,1024]{1,0:T(8,128)}, s32[8,2]{0,1:T(2,128)S(1)}, f32[8,128,128]{2,1,0:T(8,128)S(1)}, s32[]{:T(128)}) %tuple.65), condition=%wide.while_cond, body=%wide.while_body.sunk | while | flops 2 | bytes 131181 | solution.py:36
  449.0 78.8 %custom-call.69 = f32[8,128,128]{1,2,0:T(8,128)S(1)} custom-call(f32[8,128,128]{2,1,0:T(8,128)S(1)} %get-tuple-element.9), custom_call_target="InvertDiagBlocksLowerTriangular" | custom-call | tf_op jit(solution)/shard_map/triangular_solve | solution.py:36
  544.2 10.1 %all-to-all-start = ((s32[128,2,1]{1,2,0:T(1,128)}), s32[128,2,1]{1,2,0:T(1,128)S(1)}, u32[]{:S(2)}, u32[]{:S(2)}) async-start(s32[128,2,1]{1,2,0:T(1,128)} %bitcast.5), calls=%async_computation | async-start | bytes 131072 | tf_op jit(solution)/shard_map/all_to_all | solution.py:32
  554.3 5.3 broadcast_in_dim.5
  559.6 19.4 %scatter_fusion = bf16[256,128,128]{2,1,0:T(8,128)(2,1)} fusion(bf16[256,128,128]{2,1,0:T(8,128)(2,1)} %broadcast_in_dim.5, s32[128]{0:T(128)S(1)} %fusion.60, bf16[128,128,128]{2,1,0:T(8,128)(2,1)} %param.10), kind=kCustom, calls=%fused_computation.1 | custom fusion | bytes 12583424 | tf_op jit(solution)/shard_map/scatter | solution.py:27
  579.0 10.4 %all-to-all-start.1 = ((bf16[256,128,128]{2,1,0:T(8,128)(2,1)}), bf16[256,128,128]{2,1,0:T(8,128)(2,1)}, u32[]{:S(2)}, u32[]{:S(2)}) async-start(bf16[256,128,128]{2,1,0:T(8,128)(2,1)} %scatter_fusion), calls=%async_computation.1 | async-start | bytes 16777216 | tf_op jit(solution)/shard_map/all_to_all | solution.py:31
  593.1 5.5 copy.30
  599.4 4.9 copy.24
  606.8 153.3 %all-to-all-done.1 = bf16[256,128,128]{2,1,0:T(8,128)(2,1)} async-done(((bf16[256,128,128]{2,1,0:T(8,128)(2,1)}), bf16[256,128,128]{2,1,0:T(8,128)(2,1)}, u32[]{:S(2)}, u32[]{:S(2)}) %all-to-all-start.1) | async-done | bytes 8388640 | tf_op jit(solution)/shard_map/all_to_all | solution.py:31
  760.1 11.2 %convert_element_type.13 = f32[256,128,128]{2,1,0:T(8,128)} convert(bf16[256,128,128]{2,1,0:T(8,128)(2,1)} %all-to-all-done.1) | non-fusion elementwise | flops 4194304 | bytes 25165824 | tf_op jit(solution)/shard_map/convert_element_type | solution.py:51
  771.4 50.4 %scatter_fusion.1 = f32[128,128,128]{2,1,0:T(8,128)} fusion(f32[128,128,128]{2,1,0:T(8,128)} %bitcast.139, s32[256]{0:T(256)S(1)} %bitcast.148, f32[256,128,128]{2,1,0:T(8,128)} %convert_element_type.13), kind=kCustom, calls=%fused_computation.2 | custom fusion | flops 4194304 | bytes 50332672 | tf_op jit(solution)/shard_map/scatter-add | solution.py:51
  821.8 13.1 %copy.26 = f32[16,128,8,128]{3,2,1,0:T(8,128)} copy(f32[16,128,8,128]{3,1,2,0:T(8,128)} %bitcast.140) | data formatting | bytes 16777216 | tf_op jit(solution)/shard_map/transpose | solution.py:54
  838.3 12.9 %fusion = f32[2048,1024]{1,0:T(8,128)} fusion(f32[256,8,8,128]{3,2,1,0:T(8,128)S(1)} %bitcast.142, f32[256,8,8,128]{3,2,1,0:T(8,128)S(1)} %bitcast.144, bf16[2048,1024]{0,1:T(8,128)(2,1)} %all-gather.5.cloned.1.call-done, bf16[1024,1024]{0,1:T(8,128)(2,1)} %all-reduce.3.cloned.1.call-done), kind=kOutput, calls=%fused_computation.6 | convolution fusion | flops 4299161600 | bytes 31457280 | tf_op jit(solution)/shard_map/dot_general | solution.py:57
  (115 shorter events, 87.5 us)
Async XLA Ops:
  7.2 198.4 %all-gather.3.cloned.1.call-start = ((), (), s32[]{:S(2)}) async-start(), calls=%async_computation.2 | async-start | bytes 4227072 | tf_op jit(solution)/shard_map/all_gather | solution.py:34
  7.9 581.8 %all-gather.5.cloned.1.call-start = ((), (), s32[]{:S(2)}) async-start(), calls=%async_computation.3 | async-start | bytes 4456448 | tf_op jit(solution)/shard_map/all_gather | solution.py:40
  215.4 1.9 copy-start
  420.6 107.2 %copy-start.2 = (f32[128,1024]{1,0:T(8,128)S(1)}, f32[128,1024]{1,0:T(8,128)}, u32[]{:S(2)}) copy-start(f32[128,1024]{1,0:T(8,128)} %param.9) | copy-start | bytes 1572868
  528.1 13.7 %copy-start.4 = (s32[128,1]{0,1:T(1,128)S(1)}, s32[128,1]{0,1:T(1,128)}, u32[]{:S(2)}) copy-start(s32[128,1]{0,1:T(1,128)} %param.11) | copy-start | bytes 1540
  544.2 34.8 %all-to-all-start = ((s32[128,2,1]{1,2,0:T(1,128)}), s32[128,2,1]{1,2,0:T(1,128)S(1)}, u32[]{:S(2)}, u32[]{:S(2)}) async-start(s32[128,2,1]{1,2,0:T(1,128)} %bitcast.5), calls=%async_computation | async-start | bytes 131072 | tf_op jit(solution)/shard_map/all_to_all | solution.py:32
  579.0 181.2 %all-to-all-start.1 = ((bf16[256,128,128]{2,1,0:T(8,128)(2,1)}), bf16[256,128,128]{2,1,0:T(8,128)(2,1)}, u32[]{:S(2)}, u32[]{:S(2)}) async-start(bf16[256,128,128]{2,1,0:T(8,128)(2,1)} %scatter_fusion), calls=%async_computation.1 | async-start | bytes 16777216 | tf_op jit(solution)/shard_map/all_to_all | solution.py:31
  589.3 245.6 %all-reduce.3.cloned.1.call-start = ((), (), s32[]{:S(2)}) async-start(), calls=%async_computation.4 | async-start | bytes 4194304 | tf_op jit(solution)/shard_map/psum | solution.py:9
  599.4 4.9 copy-start.3
  834.9 3.4 copy-start.1
Sparse Core Ops, SparseCore 0:
  9.7 195.8 all-gather.2
  541.9 45.7 all-gather.4
  593.2 168.8 all-reduce.2
where the time goes:
time: 869 us; the launch traced here: 858 us
  waiting for transfers between devices  352 us (41%)
  other arithmetic  328 us (38%)
  local copies, waits for them, and re-layouts  89.1 us (10%)
  matrix products  49.1 us (6%)
  starting transfers between devices  20.8 us (2%)
  between operations  19.6 us (2%)
    all_gather x1, waiting for transfers between devices, per_device(): pivot_whole = lax.all_gather(pivot, ('row', 'col'), axis=0, tiled=True)  198 us
    another operation x30, other arithmetic, per_device(): lower_factor = jnp.linalg.cholesky(pivot_whole)  173 us
    all_to_all x1, waiting for transfers between devices, per_device(): lax.all_to_all(outgoing, ('row', 'col'), split_axis=0, concat_axis=0, til...  153 us
    another operation x3, other arithmetic, per_device(): lax.linalg.triangular_solve(lower_factor, panel, left_side=False, lower=T...  83.7 us
    scatter-add x1, other arithmetic, per_device(): tiles = tiles.at[spots].add(arrived.astype(jnp.float32), mode='drop')  50.4 us
    another operation x24, local copies, waits for them, and re-layouts  23.3 us
    another operation x14, matrix products, per_device(): lower_factor = jnp.linalg.cholesky(pivot_whole)  23.1 us
    scatter x1, local copies, waits for them, and re-layouts, per_device(): jnp.zeros((devices * capacity, side, side), jnp.bfloat16).at[target]  19.4 us
  transfers between devices with their start and end apart: 5, of which 2 were waited for; matrix products, arithmetic and copies ran while one was open for 14% of the time, Pallas kernels for 0%

commit v1 on v0

v1 whole, which is shorter than its diff:
```python
import jax
import jax.numpy as jnp
from jax import lax
from jax.experimental import pallas as pl
from jax.experimental.pallas import tpu as pltpu
from jax.sharding import PartitionSpec as P

SIDE = 128
SUB = 8
HIGHEST = lax.Precision.HIGHEST
MESH = pl.DeviceIdType.MESH
VMEM = pltpu.VMEM
HBM = pltpu.HBM
CONTRACT_LAST = (((1,), (1,)), ((), ()))


def coordinates():
    row, col = lax.axis_index("row"), lax.axis_index("col")
    return {
        "y": row // 2,
        "x": (row % 2) * 2 + (col // 2) % 2,
        "z": col // 4,
        "core": col % 2,
    }


def mesh_index(at):
    return (at["y"] * 2 + at["x"] // 2, at["z"] * 4 + (at["x"] % 2) * 2 + at["core"])


def pack_kernel(dest_ref, blocks_ref, out_ref, count, sem):
    devices = count.shape[0]
    number = blocks_ref.shape[0]

    @pl.loop(0, devices)
    def _(d):
        count[d] = 0

    @pl.loop(0, number)
    def _(i):
        owner = dest_ref[i]
        used = count[owner]
        count[owner] = used + 1
        pltpu.make_async_copy(blocks_ref.at[i], out_ref.at[owner * 2 + used], sem).start()

    pltpu.make_async_copy(blocks_ref, blocks_ref, sem).wait()


def pack(dest, blocks, devices):
    number, side, _ = blocks.shape
    return pl.pallas_call(
        pack_kernel,
        out_shape=jax.ShapeDtypeStruct((2 * devices, side, side), blocks.dtype),
        grid_spec=pltpu.PrefetchScalarGridSpec(
            num_scalar_prefetch=1,
            grid=(),
            in_specs=[pl.BlockSpec(memory_space=VMEM)],
            out_specs=pl.BlockSpec(memory_space=HBM),
            scratch_shapes=[pltpu.SMEM((devices,), jnp.int32), pltpu.SemaphoreType.DMA],
        ),
        name="pack",
    )(dest, blocks)


ORDERS = (("x", "y", "z"), ("y", "z", "x"), ("z", "x", "y"))


def gather_kernel(piece_bounds, own_ref, out_ref, local_sem, send_sem, recv_sem, pair_send, pair_recv):
    me = coordinates()
    pieces = range(len(ORDERS))
    first = {
        "y": me["y"], "xh": me["x"] // 2, "z": me["z"], "xl": me["x"] % 2, "core": me["core"],
    }

    def view(done, piece):
        low, high = piece_bounds[piece]
        pick = lambda name, axis: slice(None) if axis in done else first[name]
        return out_ref.at[
            pick("y", "y"), pick("xh", "x"), pick("z", "z"), pick("xl", "x"), first["core"], :, pl.ds(low, high - low)
        ]

    own = out_ref.at[first["y"], first["xh"], first["z"], first["xl"], first["core"]]
    copy = pltpu.make_async_copy(own_ref, own, local_sem)
    copy.start()

    def send(piece, stage, turn):
        done, axis = ORDERS[piece][:stage], ORDERS[piece][stage]
        at = dict(me)
        at[axis] = jnp.bitwise_xor(me[axis], turn)
        low, high = piece_bounds[piece]
        source = own_ref.at[:, pl.ds(low, high - low)] if stage == 0 else view(done, piece)
        return pltpu.make_async_remote_copy(
            src_ref=source,
            dst_ref=view(done, piece),
            send_sem=send_sem.at[piece, stage, turn - 1],
            recv_sem=recv_sem.at[piece, stage, turn - 1],
            device_id=mesh_index(at),
            device_id_type=MESH,
        )

    def pair(piece, stage):
        at = dict(me)
        at["core"] = 1 - me["core"]
        ref = view(ORDERS[piece][:stage], piece)
        return pltpu.make_async_remote_copy(
            src_ref=ref, dst_ref=ref, send_sem=pair_send.at[piece], recv_sem=pair_recv.at[piece],
            device_id=mesh_index(at), device_id_type=MESH,
        )

    turns = (1, 3, 2)
    for piece in pieces:
        for turn in turns:
            send(piece, 0, turn).start()
    copy.wait()
    for stage in (1, 2):
        for piece in pieces:
            for turn in turns:
                send(piece, stage - 1, turn).wait_recv()
            for turn in turns:
                send(piece, stage, turn).start()
    for piece in pieces:
        for turn in turns:
            send(piece, 2, turn).wait_recv()
        pair(piece, 3).start()
    for piece in pieces:
        for stage in range(3):
            for turn in turns:
                send(piece, stage, turn).wait_send()
        pair(piece, 3).wait()


def gather(own):
    rows, width = own.shape
    third = (width // SIDE // 3) * SIDE
    bounds = ((0, third), (third, 2 * third), (2 * third, width))
    count = len(ORDERS)

    def kernel(*refs):
        gather_kernel(bounds, *refs)

    out = pl.pallas_call(
        kernel,
        out_shape=jax.ShapeDtypeStruct((4, 2, 4, 2, 2, rows, width), own.dtype),
        in_specs=[pl.BlockSpec(memory_space=HBM)],
        out_specs=pl.BlockSpec(memory_space=HBM),
        scratch_shapes=[
            pltpu.SemaphoreType.DMA,
            pltpu.SemaphoreType.DMA((count, 3, 3)),
            pltpu.SemaphoreType.DMA((count, 3, 3)),
            pltpu.SemaphoreType.DMA((count,)),
            pltpu.SemaphoreType.DMA((count,)),
        ],
        compiler_params=pltpu.CompilerParams(has_side_effects=True),
        name="pivot_gather",
    )(own)
    return out.reshape(128 * rows, width)


def factor_block(load, store):
    groups = SIDE // SUB
    block = [load(h) for h in range(groups)]
    rows = lax.broadcasted_iota(jnp.int32, (SUB, SIDE), 0)
    cols = lax.broadcasted_iota(jnp.int32, (SUB, SIDE), 1)
    inverse = [jnp.where(cols == rows + SUB * h, 1.0, 0.0).astype(jnp.float32) for h in range(groups)]

    def spread_row(value, r):
        return jnp.broadcast_to(value[r : r + 1, :], (SUB, SIDE))

    def spread_column(value, c):
        return jnp.broadcast_to(value[:, c : c + 1], (SUB, SIDE))

    for g in range(groups):
        heads = [spread_column(block[g], SUB * g + j) for j in range(SUB)]
        corner = {(i, j): spread_row(heads[j], i) for j in range(SUB) for i in range(j, SUB)}
        upper = [spread_row(block[g], i) for i in range(SUB)]
        lower = [spread_row(inverse[g], i) for i in range(SUB)]
        below = {h: [spread_column(block[h], SUB * g + j) for j in range(SUB)] for h in range(g + 1, groups)}
        for j in range(SUB):
            scale = lax.rsqrt(corner[j, j])
            column = {i: corner[i, j] * scale for i in range(j + 1, SUB)}
            for i in range(j + 1, SUB):
                for k in range(j + 1, i + 1):
                    corner[i, k] = corner[i, k] - column[i] * column[k]
            u = upper[j] * scale
            w = lower[j] * scale
            for i in range(j + 1, SUB):
                upper[i] = upper[i] - column[i] * u
                lower[i] = lower[i] - column[i] * w
            for h in range(g + 1, groups):
                entry = below[h][j] * scale
                for i in range(j + 1, SUB):
                    below[h][i] = below[h][i] - entry * column[i]
                block[h] = block[h] - entry * u
                inverse[h] = inverse[h] - entry * w
            store(SUB * g + j, w[0:1, :])


def cholesky_kernel(pivot_ref, panel_ref, factor_ref, rounded_ref, work, solved, inverse):
    size = factor_ref.shape[1]
    own = panel_ref.shape[0]
    blocks = size // SIDE
    work[pl.ds(0, size), :] = pivot_ref[:, pl.ds(0, size)]
    work[pl.ds(size, own), :] = panel_ref[...]

    @pl.loop(0, blocks)
    def _(k):
        start = pl.multiple_of(k * SIDE, SIDE)
        columns = pl.ds(start, SIDE)

        def load(h):
            return work[pl.ds(pl.multiple_of(start + SUB * h, SUB), SUB), columns]

        def store(r, value):
            inverse[r : r + 1, :] = value

        factor_block(load, store)
        solved[...] = lax.dot_general(
            work[:, columns], inverse[...], CONTRACT_LAST, precision=HIGHEST, preferred_element_type=jnp.float32
        )
        mine = solved[pl.ds(size, own), :]
        factor_ref[:, columns] = mine
        rounded_ref[:, columns] = mine.astype(jnp.bfloat16)

        @pl.loop(k + 1, blocks)
        def _(j):
            there = pl.multiple_of(j * SIDE, SIDE)
            work[:, pl.ds(there, SIDE)] = work[:, pl.ds(there, SIDE)] - lax.dot_general(
                solved[...], solved[pl.ds(there, SIDE), :], CONTRACT_LAST,
                precision=HIGHEST, preferred_element_type=jnp.float32,
            )


def cholesky_solve(pivot, panel):
    own, size = panel.shape
    return pl.pallas_call(
        cholesky_kernel,
        out_shape=(jax.ShapeDtypeStruct((own, size), jnp.float32), jax.ShapeDtypeStruct((own, size), jnp.bfloat16)),
        in_specs=[pl.BlockSpec(memory_space=VMEM)] * 2,
        out_specs=(pl.BlockSpec(memory_space=VMEM),) * 2,
        scratch_shapes=[
            VMEM((size + own, size), jnp.float32), VMEM((size + own, SIDE), jnp.float32), VMEM((SIDE, SIDE), jnp.float32),
        ],
        compiler_params=pltpu.CompilerParams(vmem_limit_bytes=30 << 20),
        cost_estimate=pl.CostEstimate(flops=10**10, bytes_accessed=10**7, transcendentals=0),
        name="cholesky_solve",
    )(pivot, panel)


def spread_kernel(own_ref, row_ref, col_ref, local_sem, row_send, row_recv, pair_send, pair_recv, col_send, col_recv):
    row, col = lax.axis_index("row"), lax.axis_index("col")
    chip, core = col // 2, col % 2
    column = row * 2 + col // 8
    pairs = row_send.shape[0]
    rows = col_send.shape[0]
    local = pltpu.make_async_copy(own_ref, row_ref.at[col], local_sem)
    local.start()

    def along(turn):
        return pltpu.make_async_remote_copy(
            src_ref=own_ref, dst_ref=row_ref.at[col],
            send_sem=row_send.at[turn - 1], recv_sem=row_recv.at[turn - 1],
            device_id=(row, jnp.bitwise_xor(chip, turn) * 2 + core), device_id_type=MESH,
        )

    def pair(turn):
        block = row_ref.at[jnp.bitwise_xor(chip, turn) * 2 + core]
        return pltpu.make_async_remote_copy(
            src_ref=own_ref if turn == 0 else block, dst_ref=block,
            send_sem=pair_send.at[turn], recv_sem=pair_recv.at[turn],
            device_id=(row, chip * 2 + 1 - core), device_id_type=MESH,
        )

    def down(turn):
        return pltpu.make_async_remote_copy(
            src_ref=own_ref, dst_ref=col_ref.at[col % 8],
            send_sem=col_send.at[turn], recv_sem=col_recv.at[col % 8],
            device_id=(jnp.bitwise_xor(row, turn), column), device_id_type=MESH,
        )

    def arrival(k):
        return pltpu.make_async_remote_copy(
            src_ref=own_ref, dst_ref=col_ref.at[k], send_sem=col_send.at[0], recv_sem=col_recv.at[k],
            device_id=(row, col), device_id_type=MESH,
        )

    for turn in range(1, pairs + 1):
        along(turn).start()
        down(turn).start()
    at_home = col == column
    @pl.when(at_home)
    def _():
        pltpu.make_async_copy(own_ref, col_ref.at[col % 8], col_recv.at[col % 8]).start()
    @pl.when(jnp.logical_not(at_home))
    def _():
        down(0).start()
    pair(0).start()
    for turn in range(1, pairs + 1):
        along(turn).wait_recv()
        pair(turn).start()
    for k in range(rows):
        arrival(k).wait_recv()
    local.wait()
    for turn in range(1, pairs + 1):
        along(turn).wait_send()
        down(turn).wait_send()
    @pl.when(jnp.logical_not(at_home))
    def _():
        down(0).wait_send()
    for turn in range(pairs + 1):
        pair(turn).wait()


def spread(rounded):
    own, size = rounded.shape
    cols, rows = lax.axis_size("col"), lax.axis_size("row")
    dma = pltpu.SemaphoreType.DMA
    row_side, col_side = pl.pallas_call(
        spread_kernel,
        out_shape=(
            jax.ShapeDtypeStruct((cols, own, size), rounded.dtype),
            jax.ShapeDtypeStruct((size // own, own, size), rounded.dtype),
        ),
        in_specs=[pl.BlockSpec(memory_space=HBM)],
        out_specs=(pl.BlockSpec(memory_space=HBM),) * 2,
        scratch_shapes=[dma, dma((7,)), dma((7,)), dma((8,)), dma((8,)), dma((rows,)), dma((8,))],
        compiler_params=pltpu.CompilerParams(has_side_effects=True),
        name="factor_spread",
    )(rounded)
    return row_side.reshape(cols * own, size), col_side.reshape(size, size)


def update_kernel(pattern_ref, front_ref, row_ref, col_ref, out_ref):
    step = pl.program_id(0)
    height, width = out_ref.shape
    product = lax.dot_general(row_ref[...], col_ref[...], CONTRACT_LAST, preferred_element_type=jnp.float32)
    for a in range(height // SIDE):
        for b in range(width // SIDE):
            here = (slice(a * SIDE, (a + 1) * SIDE), slice(b * SIDE, (b + 1) * SIDE))
            keep = pattern_ref[step * (height // SIDE) + a, b].astype(jnp.float32)
            out_ref[here] = front_ref[here] - product[here] * keep


def trailing(pattern, front, row_side, col_side):
    tile_rows, tile_cols = front.shape
    size = row_side.shape[1]
    height = 256
    return pl.pallas_call(
        update_kernel,
        out_shape=jax.ShapeDtypeStruct(front.shape, jnp.float32),
        grid_spec=pltpu.PrefetchScalarGridSpec(
            num_scalar_prefetch=1,
            grid=(tile_rows // height,),
            in_specs=[
                pl.BlockSpec((height, tile_cols), lambda i, p: (i, 0)),
                pl.BlockSpec((height, size), lambda i, p: (i, 0)),
                pl.BlockSpec((tile_cols, size), lambda i, p: (0, 0)),
            ],
            out_specs=pl.BlockSpec((height, tile_cols), lambda i, p: (i, 0)),
        ),
        compiler_params=pltpu.CompilerParams(vmem_limit_bytes=30 << 20),
        cost_estimate=pl.CostEstimate(flops=2 * tile_rows * tile_cols * size, bytes_accessed=24 << 20, transcendentals=0),
        name="trailing",
    )(pattern, front, row_side, col_side)


def extend_kernel(place_ref, base_ref, arrived_ref, out_ref, tile, slots, load_sem, slot_sem, out_sem):
    total = arrived_ref.shape[0]
    chunk = slots.shape[1]
    steps = total // chunk
    block_cols = tile.shape[1] // SIDE
    blocks = (tile.shape[0] // SIDE) * block_cols

    def fetch(c):
        return pltpu.make_async_copy(arrived_ref.at[pl.ds(c * chunk, chunk)], slots.at[c % 2], slot_sem.at[c % 2])

    load = pltpu.make_async_copy(base_ref, tile, load_sem)
    load.start()
    fetch(0).start()
    load.wait()
    for c in range(steps):
        if c + 1 < steps:
            fetch(c + 1).start()
        fetch(c).wait()

        @pl.loop(0, chunk)
        def _(n):
            place = place_ref[c * chunk + n]

            @pl.when(place < blocks)
            def _():
                top = pl.multiple_of((place // block_cols) * SIDE, SIDE)
                left = pl.multiple_of((place % block_cols) * SIDE, SIDE)
                here = (pl.ds(top, SIDE), pl.ds(left, SIDE))
                tile[here] = tile[here] + slots[c % 2, n].astype(jnp.float32)

    store = pltpu.make_async_copy(tile, out_ref, out_sem)
    store.start()
    store.wait()


def extend_add(places, base, arrived):
    dma = pltpu.SemaphoreType.DMA
    return pl.pallas_call(
        extend_kernel,
        out_shape=jax.ShapeDtypeStruct(base.shape, base.dtype),
        grid_spec=pltpu.PrefetchScalarGridSpec(
            num_scalar_prefetch=1,
            grid=(),
            in_specs=[pl.BlockSpec(memory_space=HBM)] * 2,
            out_specs=pl.BlockSpec(memory_space=HBM),
            scratch_shapes=[
                VMEM(base.shape, jnp.float32), VMEM((2, 32, SIDE, SIDE), arrived.dtype), dma, dma((2,)), dma,
            ],
        ),
        compiler_params=pltpu.CompilerParams(vmem_limit_bytes=20 << 20),
        name="extend_add",
    )(places, base, arrived)


def arrivals(dest, pos, me, blocks):
    lane = lax.broadcasted_iota(jnp.int32, dest.shape, 1)
    mine = dest == me
    first = jnp.min(jnp.where(mine, lane, dest.shape[1]), axis=1)
    last = jnp.max(jnp.where(mine, lane, -1), axis=1)
    place_first = jnp.sum(jnp.where(lane == first[:, None], pos, 0), axis=1)
    place_last = jnp.sum(jnp.where(lane == last[:, None], pos, 0), axis=1)
    place_first = jnp.where(last >= 0, place_first, blocks)
    place_last = jnp.where(last > first, place_last, blocks)
    return jnp.stack([place_first, place_last], axis=1).reshape(-1)


def per_device(front, pivot, panel, child_blocks, child_dest, child_pos, pattern):
    devices = lax.axis_size("row") * lax.axis_size("col")
    me = lax.axis_index("row") * lax.axis_size("col") + lax.axis_index("col")
    size = panel.shape[1]
    dest = child_dest[:, 0]
    outgoing = pack(dest, child_blocks, devices)
    arrived = lax.all_to_all(outgoing, ("row", "col"), split_axis=0, concat_axis=0, tiled=True)
    notes = jnp.concatenate([dest[None], child_pos[None], jnp.zeros((6, dest.shape[0]), jnp.int32)], axis=0)
    everything = gather(jnp.concatenate([pivot, notes.astype(jnp.float32)], axis=1))
    factor, rounded = cholesky_solve(everything, panel)
    row_side, col_side = spread(rounded)
    base = trailing(pattern, front, row_side, col_side)
    told = everything[:, size:].reshape(devices, 8, -1).astype(jnp.int32)
    tile_blocks = (front.shape[0] // SIDE) * (front.shape[1] // SIDE)
    places = arrivals(told[:, 0], told[:, 1], me, tile_blocks)
    schur = extend_add(places, base, arrived)
    return (schur, factor)


def solution(mesh):
    return jax.shard_map(
        per_device,
        mesh=mesh,
        in_specs=(
            P("row", "col"),
            P(("row", "col"), None),
            P(("row", "col"), None),
            P(("row", "col"), None, None),
            P(("row", "col"), None),
            P(("row", "col")),
            P("row", "col"),
        ),
        out_specs=(P("row", "col"), P(("row", "col"), None)),
        check_vma=False,
    )
```

time: 869 us -> 326 us (0.38)
  the two profiles are of different devices: /device:TPU:92 before, /device:TPU:1 now
where the time goes in v1:
time: 326 us
  Pallas kernels  293 us (90%)
  local copies, waits for them, and re-layouts  17.5 us (5%)
  starting transfers between devices  11.9 us (4%)
    pallas_call x1, Pallas kernels, gather(): pl.pallas_call(kernel, out_shape=jax.ShapeDtypeStruct((4, 2, 4, 2, 2, row...  125 us
    pallas_call x1, Pallas kernels, spread(): pl.pallas_call(spread_kernel, out_shape=(jax.ShapeDtypeStruct((cols, own,...  82.4 us
    pallas_call x1, Pallas kernels, cholesky_solve(): pl.pallas_call(cholesky_kernel, out_shape=(jax.ShapeDtypeStruct((own, siz...  61.5 us
    unnamed x25, local copies, waits for them, and re-layouts  17.1 us
    pallas_call x1, Pallas kernels, extend_add(): pl.pallas_call(extend_kernel, out_shape=jax.ShapeDtypeStruct(base.shape,...  13.1 us
    all_to_all x1, starting transfers between devices, per_device(): lax.all_to_all(outgoing, ('row', 'col'), split_axis=0, concat_axis=0, til...  11.9 us
    pallas_call x1, Pallas kernels, trailing(): pl.pallas_call(update_kernel, out_shape=jax.ShapeDtypeStruct(front.shape,...  6.71 us
  transfers between devices with their start and end apart: 1, of which 0 were waited for; matrix products, arithmetic and copies ran while one was open for 1% of the time, Pallas kernels for 85%

profile of v1, /device:TPU:1, one launch (start us, length us, event | category | flops | bytes accessed | tf_op | source)
XLA Modules:
  0.0 325.8 jit_solution(14462773604125796438)
XLA Ops:
  0.6 4.9 %pack.1 = bf16[256,128,128]{2,1,0:T(8,128)(2,1)} custom-call(s32[128]{0:T(128)} %bitcast.23, bf16[128,128,128]{2,1,0:T(8,128)(2,1)} %blocks_ref.1), custom_call_target="tpu_custom_call" | custom-call | tf_op jit(solution)/shard_map/pack/pallas_call | solution.py:51
  5.5 0.0 copy-start.9
  5.5 0.0 copy-start.10
  5.5 0.0 copy-start.11
  5.6 0.0 copy-start.8
  5.6 0.0 copy-start.7
  5.6 11.9 %all-to-all-start = ((bf16[256,128,128]{2,1,0:T(8,128)(2,1)}), bf16[256,128,128]{2,1,0:T(8,128)(2,1)}, u32[]{:S(2)}, u32[]{:S(2)}) async-start(bf16[256,128,128]{2,1,0:T(8,128)(2,1)} %pack.1), calls=%async_computation | async-start | bytes 16777216 | tf_op jit(solution)/shard_map/all_to_all | solution.py:438
  17.5 0.1 pad.6.clone
  17.6 0.1 copy.12.pattern_ref
  17.7 0.1 add_convert_fusion
  17.8 0.6 pad_maximum_fusion.refs_0_
  18.4 124.9 %pivot_gather.1 = f32[4,2,4,2,2,8,1152]{6,5,4,3,2,1,0:T(8,128)} custom-call(f32[8,1152]{1,0:T(8,128)} %pad_maximum_fusion.refs_0_), custom_call_target="tpu_custom_call" | custom-call | tf_op jit(solution)/shard_map/pivot_gather/pallas_call | solution.py:141
  143.3 1.1 fusion
  144.4 0.1 fusion.3
  144.5 0.1 select_reduce_fusion.2
  144.6 0.2 select_reduce_fusion.1
  144.8 0.1 copy.11
  144.9 0.1 reshape.62.place_ref
  145.1 2.3 copy-done.3
  147.4 61.5 %cholesky_solve.1 = (f32[128,1024]{1,0:T(8,128)}, bf16[128,1024]{1,0:T(8,128)(2,1)S(1)}) custom-call(f32[1024,1152]{1,0:T(8,128)S(1)} %bitcast.18, f32[128,1024]{1,0:T(8,128)S(1)} %copy-done.7), custom_call_target="tpu_custom_call" | custom-call | flops 10000000000 | bytes 10000000 | tf_op jit(solution)/shard_map/cholesky_solve/pallas_call | solution.py:235
  208.9 0.7 copy-done.6
  209.6 82.4 %factor_spread.1 = (bf16[16,128,1024]{2,1,0:T(8,128)(2,1)}, bf16[8,128,1024]{2,1,0:T(8,128)(2,1)}) custom-call(bf16[128,1024]{1,0:T(8,128)(2,1)} %copy-done.6), custom_call_target="tpu_custom_call" | custom-call | tf_op jit(solution)/shard_map/factor_spread/pallas_call | solution.py:317
  292.0 0.0 copy-start.2
  292.0 3.4 %copy-done.2 = f32[2048,1024]{1,0:T(8,128)S(1)} copy-done((f32[2048,1024]{1,0:T(8,128)S(1)}, f32[2048,1024]{1,0:T(8,128)}, u32[]{:S(2)}) %copy-start.2) | copy-done | bytes 8388632
  295.4 2.2 copy-done.4
  297.5 1.6 copy-done.5
  299.1 6.7 %trailing.1.base_ref = f32[2048,1024]{1,0:T(8,128)S(1)} custom-call(s32[16,8]{1,0:T(8,128)S(1)} %copy.12.pattern_ref, f32[2048,1024]{1,0:T(8,128)S(1)} %copy-done.2, bf16[2048,1024]{1,0:T(8,128)(2,1)S(1)} %bitcast.19, bf16[1024,1024]{1,0:T(8,128)(2,1)S(1)} %bitcast.20), custom_call_target="tpu_custom_call" | custom-call | flops 4294967296 | bytes 25165824 | tf_op jit(solution)/shard_map/trailing/pallas_call | solution.py:347
  305.8 0.0 copy-start
  305.9 3.4 %copy-done = f32[2048,1024]{1,0:T(8,128)} copy-done((f32[2048,1024]{1,0:T(8,128)}, f32[2048,1024]{1,0:T(8,128)S(1)}, u32[]{:S(2)}) %copy-start) | copy-done | bytes 8388632
  309.2 0.0 all-to-all-done.arrived_ref
  309.3 3.4 %copy-done.1 = f32[2048,1024]{1,0:T(8,128)S(1)} copy-done((f32[2048,1024]{1,0:T(8,128)S(1)}, f32[2048,1024]{1,0:T(8,128)}, u32[]{:S(2)}) %copy-start.1) | copy-done | bytes 8388632
  312.6 13.1 %extend_add.1 = f32[2048,1024]{1,0:T(8,128)} custom-call(s32[256]{0:T(256)S(1)} %reshape.62.place_ref, f32[2048,1024]{1,0:T(8,128)S(1)} %copy-done.1, bf16[256,128,128]{2,1,0:T(8,128)(2,1)} %all-to-all-done.arrived_ref), custom_call_target="tpu_custom_call" | custom-call | tf_op jit(solution)/shard_map/extend_add/pallas_call | solution.py:403
  (13 shorter events, 0.0 us)
Async XLA Ops:
  5.5 12.1 %copy-start.9 = (s32[16,8]{0,1:T(8,128)S(1)}, s32[16,8]{0,1:T(8,128)}, u32[]{:S(2)}) copy-start(s32[16,8]{0,1:T(8,128)} %param.13) | copy-start | bytes 1540
  5.5 12.2 %copy-start.10 = (s32[128,1]{0,1:T(1,128)S(1)}, s32[128,1]{0,1:T(1,128)}, u32[]{:S(2)}) copy-start(s32[128,1]{0,1:T(1,128)} %param.11) | copy-start | bytes 1540
  5.5 12.1 %copy-start.11 = (s32[128]{0:T(128)S(1)}, s32[128]{0:T(128)}, u32[]{:S(2)}) copy-start(s32[128]{0:T(128)} %param.12) | copy-start | bytes 1540
  5.6 12.2 %copy-start.8 = (f32[8,1024]{1,0:T(8,128)S(1)}, f32[8,1024]{1,0:T(8,128)}, u32[]{:S(2)}) copy-start(f32[8,1024]{1,0:T(8,128)} %param.8) | copy-start | bytes 98308
  5.6 139.5 %copy-start.7 = (f32[128,1024]{1,0:T(8,128)S(1)}, f32[128,1024]{1,0:T(8,128)}, u32[]{:S(2)}) copy-start(f32[128,1024]{1,0:T(8,128)} %panel_ref.1) | copy-start | bytes 1572868
  5.6 303.7 %all-to-all-start = ((bf16[256,128,128]{2,1,0:T(8,128)(2,1)}), bf16[256,128,128]{2,1,0:T(8,128)(2,1)}, u32[]{:S(2)}, u32[]{:S(2)}) async-start(bf16[256,128,128]{2,1,0:T(8,128)(2,1)} %pack.1), calls=%async_computation | async-start | bytes 16777216 | tf_op jit(solution)/shard_map/all_to_all | solution.py:438
  145.1 2.3 copy-start.3
  208.9 0.7 copy-start.6
  292.0 3.4 %copy-start.2 = (f32[2048,1024]{1,0:T(8,128)S(1)}, f32[2048,1024]{1,0:T(8,128)}, u32[]{:S(2)}) copy-start(f32[2048,1024]{1,0:T(8,128)} %front_ref.1) | copy-start | bytes 25165828
  295.4 2.2 copy-start.4
  297.5 1.6 copy-start.5
  305.8 3.4 %copy-start = (f32[2048,1024]{1,0:T(8,128)}, f32[2048,1024]{1,0:T(8,128)S(1)}, u32[]{:S(2)}) copy-start(f32[2048,1024]{1,0:T(8,128)S(1)} %trailing.1.base_ref) | copy-start | bytes 25165828
  309.3 3.4 %copy-start.1 = (f32[2048,1024]{1,0:T(8,128)S(1)}, f32[2048,1024]{1,0:T(8,128)}, u32[]{:S(2)}) copy-start(f32[2048,1024]{1,0:T(8,128)} %copy-done) | copy-start | bytes 25165828

commit v2 on v1

v2 whole, which is shorter than its diff:
```python
import jax
import jax.numpy as jnp
from jax import lax
from jax.experimental import pallas as pl
from jax.experimental.pallas import tpu as pltpu
from jax.sharding import PartitionSpec as P

SIDE = 128
SUB = 8
HIGHEST = lax.Precision.HIGHEST
MESH = pl.DeviceIdType.MESH
VMEM = pltpu.VMEM
HBM = pltpu.HBM
CONTRACT_LAST = (((1,), (1,)), ((), ()))


def coordinates():
    row, col = lax.axis_index("row"), lax.axis_index("col")
    return {
        "y": row // 2,
        "x": (row % 2) * 2 + (col // 2) % 2,
        "z": col // 4,
        "core": col % 2,
    }


def mesh_index(at):
    return (at["y"] * 2 + at["x"] // 2, at["z"] * 4 + (at["x"] % 2) * 2 + at["core"])


def pack_kernel(dest_ref, blocks_ref, out_ref, count, sem):
    devices = count.shape[0]
    number = blocks_ref.shape[0]

    @pl.loop(0, devices)
    def _(d):
        count[d] = 0

    @pl.loop(0, number)
    def _(i):
        owner = dest_ref[i]
        used = count[owner]
        count[owner] = used + 1
        pltpu.make_async_copy(blocks_ref.at[i], out_ref.at[owner * 2 + used], sem).start()

    pltpu.make_async_copy(blocks_ref, blocks_ref, sem).wait()


def pack(dest, blocks, devices):
    number, side, _ = blocks.shape
    return pl.pallas_call(
        pack_kernel,
        out_shape=jax.ShapeDtypeStruct((2 * devices, side, side), blocks.dtype),
        grid_spec=pltpu.PrefetchScalarGridSpec(
            num_scalar_prefetch=1,
            grid=(),
            in_specs=[pl.BlockSpec(memory_space=VMEM)],
            out_specs=pl.BlockSpec(memory_space=HBM),
            scratch_shapes=[pltpu.SMEM((devices,), jnp.int32), pltpu.SemaphoreType.DMA],
        ),
        name="pack",
    )(dest, blocks)


ORDERS = (("x", "y", "z"), ("y", "z", "x"), ("z", "x", "y"))
RING = 4


def gather_kernel(piece_bounds, own_ref, out_ref, local_sem, send_sem, recv_sem, ring_send, ring_recv, pair_send, pair_recv):
    me = coordinates()
    pieces = range(len(ORDERS))

    def view(piece, done, at, part=None):
        low, high = piece_bounds[piece] if part is None else part
        pick = lambda value, axis: slice(None) if axis in done else value
        return out_ref.at[
            pick(at["y"], "y"), pick(at["x"] // 2, "x"), pick(at["z"], "z"), pick(at["x"] % 2, "x"), me["core"],
            :, pl.ds(low, high - low),
        ]

    def moved(axis, value):
        at = dict(me)
        at[axis] = value
        return at

    copy = pltpu.make_async_copy(own_ref, out_ref.at[me["y"], me["x"] // 2, me["z"], me["x"] % 2, me["core"]], local_sem)
    copy.start()

    def send(piece, stage, turn):
        done, axis = ORDERS[piece][:stage], ORDERS[piece][stage]
        low, high = piece_bounds[piece]
        there = view(piece, done, me)
        return pltpu.make_async_remote_copy(
            src_ref=own_ref.at[:, pl.ds(low, high - low)] if stage == 0 else there,
            dst_ref=there,
            send_sem=send_sem.at[piece, stage, turn - 1],
            recv_sem=recv_sem.at[piece, stage, turn - 1],
            device_id=mesh_index(moved(axis, jnp.bitwise_xor(me[axis], turn))),
            device_id_type=MESH,
        )

    def ring(piece, step):
        done, axis = ORDERS[piece][:2], ORDERS[piece][2]
        low, high = piece_bounds[piece]
        cut = low + ((high - low) // SIDE * 2 // 3) * SIDE
        up, down = (me[axis] + 1) % RING, (me[axis] + RING - 1) % RING
        origin, target, part = (
            (me[axis], up, (low, high)), (me[axis], down, (low, high)), (down, up, (low, cut)), (up, down, (cut, high)),
        )[step]
        ref = view(piece, done, moved(axis, origin), part)
        return pltpu.make_async_remote_copy(
            src_ref=ref, dst_ref=ref, send_sem=ring_send.at[piece, step], recv_sem=ring_recv.at[piece, step],
            device_id=mesh_index(moved(axis, target)), device_id_type=MESH,
        )

    def pair(piece, step):
        done, axis = ORDERS[piece][:2], ORDERS[piece][2]
        ref = view(piece, done, moved(axis, (me[axis] + (0, RING - 1, 1, 2)[step]) % RING))
        return pltpu.make_async_remote_copy(
            src_ref=ref, dst_ref=ref, send_sem=pair_send.at[piece, step], recv_sem=pair_recv.at[piece, step],
            device_id=mesh_index(moved("core", 1 - me["core"])), device_id_type=MESH,
        )

    turns = (1, 3, 2)
    for piece in pieces:
        for turn in turns:
            send(piece, 0, turn).start()
    copy.wait()
    for piece in pieces:
        for turn in turns:
            send(piece, 0, turn).wait_recv()
        for turn in turns:
            send(piece, 1, turn).start()
    for piece in pieces:
        for turn in turns:
            send(piece, 1, turn).wait_recv()
        ring(piece, 0).start()
        ring(piece, 1).start()
        pair(piece, 0).start()
    for piece in pieces:
        for step in (0, 1):
            ring(piece, step).wait_recv()
            ring(piece, step + 2).start()
            pair(piece, step + 1).start()
    for piece in pieces:
        ring(piece, 2).wait_recv()
        ring(piece, 3).wait_recv()
        pair(piece, 3).start()
    for piece in pieces:
        for turn in turns:
            send(piece, 0, turn).wait_send()
            send(piece, 1, turn).wait_send()
        for step in range(4):
            ring(piece, step).wait_send()
            pair(piece, step).wait()


def gather(own):
    rows, width = own.shape
    third = (width // SIDE // 3) * SIDE
    bounds = ((0, third), (third, 2 * third), (2 * third, width))
    count = len(ORDERS)
    dma = pltpu.SemaphoreType.DMA

    def kernel(*refs):
        gather_kernel(bounds, *refs)

    out = pl.pallas_call(
        kernel,
        out_shape=jax.ShapeDtypeStruct((4, 2, 4, 2, 2, rows, width), own.dtype),
        in_specs=[pl.BlockSpec(memory_space=HBM)],
        out_specs=pl.BlockSpec(memory_space=HBM),
        scratch_shapes=[
            dma, dma((count, 2, 3)), dma((count, 2, 3)), dma((count, 4)), dma((count, 4)), dma((count, 4)), dma((count, 4)),
        ],
        compiler_params=pltpu.CompilerParams(has_side_effects=True),
        name="pivot_gather",
    )(own)
    return out.reshape(128 * rows, width)


def factor_block(load, store):
    groups = SIDE // SUB
    block = [load(h) for h in range(groups)]
    rows = lax.broadcasted_iota(jnp.int32, (SUB, SIDE), 0)
    cols = lax.broadcasted_iota(jnp.int32, (SUB, SIDE), 1)
    inverse = [jnp.where(cols == rows + SUB * h, 1.0, 0.0).astype(jnp.float32) for h in range(groups)]

    def spread_row(value, r):
        return jnp.broadcast_to(value[r : r + 1, :], (SUB, SIDE))

    def spread_column(value, c):
        return jnp.broadcast_to(value[:, c : c + 1], (SUB, SIDE))

    for g in range(groups):
        heads = [spread_column(block[g], SUB * g + j) for j in range(SUB)]
        corner = {(i, j): spread_row(heads[j], i) for j in range(SUB) for i in range(j, SUB)}
        upper = [spread_row(block[g], i) for i in range(SUB)]
        lower = [spread_row(inverse[g], i) for i in range(SUB)]
        below = {h: [spread_column(block[h], SUB * g + j) for j in range(SUB)] for h in range(g + 1, groups)}
        for j in range(SUB):
            scale = lax.rsqrt(corner[j, j])
            column = {i: corner[i, j] * scale for i in range(j + 1, SUB)}
            for i in range(j + 1, SUB):
                for k in range(j + 1, i + 1):
                    corner[i, k] = corner[i, k] - column[i] * column[k]
            u = upper[j] * scale
            w = lower[j] * scale
            for i in range(j + 1, SUB):
                upper[i] = upper[i] - column[i] * u
                lower[i] = lower[i] - column[i] * w
            for h in range(g + 1, groups):
                entry = below[h][j] * scale
                for i in range(j + 1, SUB):
                    below[h][i] = below[h][i] - entry * column[i]
                block[h] = block[h] - entry * u
                inverse[h] = inverse[h] - entry * w
            store(SUB * g + j, w[0:1, :])


def cholesky_kernel(pivot_ref, panel_ref, factor_ref, rounded_ref, work, solved, inverse):
    size = factor_ref.shape[1]
    own = panel_ref.shape[0]
    blocks = size // SIDE
    work[pl.ds(0, size), :] = pivot_ref[:, pl.ds(0, size)]
    work[pl.ds(size, own), :] = panel_ref[...]

    @pl.loop(0, blocks)
    def _(k):
        start = pl.multiple_of(k * SIDE, SIDE)
        columns = pl.ds(start, SIDE)

        def load(h):
            return work[pl.ds(pl.multiple_of(start + SUB * h, SUB), SUB), columns]

        def store(r, value):
            inverse[r : r + 1, :] = value

        factor_block(load, store)
        solved[...] = lax.dot_general(
            work[:, columns], inverse[...], CONTRACT_LAST, precision=HIGHEST, preferred_element_type=jnp.float32
        )
        mine = solved[pl.ds(size, own), :]
        factor_ref[:, columns] = mine
        rounded_ref[:, columns] = mine.astype(jnp.bfloat16)

        @pl.loop(k + 1, blocks)
        def _(j):
            there = pl.multiple_of(j * SIDE, SIDE)
            work[:, pl.ds(there, SIDE)] = work[:, pl.ds(there, SIDE)] - lax.dot_general(
                solved[...], solved[pl.ds(there, SIDE), :], CONTRACT_LAST,
                precision=HIGHEST, preferred_element_type=jnp.float32,
            )


def cholesky_solve(pivot, panel):
    own, size = panel.shape
    return pl.pallas_call(
        cholesky_kernel,
        out_shape=(jax.ShapeDtypeStruct((own, size), jnp.float32), jax.ShapeDtypeStruct((own, size), jnp.bfloat16)),
        in_specs=[pl.BlockSpec(memory_space=VMEM)] * 2,
        out_specs=(pl.BlockSpec(memory_space=VMEM),) * 2,
        scratch_shapes=[
            VMEM((size + own, size), jnp.float32), VMEM((size + own, SIDE), jnp.float32), VMEM((SIDE, SIDE), jnp.float32),
        ],
        compiler_params=pltpu.CompilerParams(vmem_limit_bytes=30 << 20),
        cost_estimate=pl.CostEstimate(flops=10**10, bytes_accessed=10**7, transcendentals=0),
        name="cholesky_solve",
    )(pivot, panel)


def spread_kernel(
    own_ref, row_ref, col_ref, local_sem, turn_send, turn_recv, send_sem, recv_sem, pair_send, pair_recv,
):
    me = coordinates()
    core = me["core"]
    row, chip = lax.axis_index("row"), lax.axis_index("col") // 2
    half = own_ref.shape[1] // 2
    sides = (
        (row_ref, "z", me["x"] % 2, lambda flip: me["x"] // 2 * 2 + flip),
        (col_ref, "y", me["x"] // 2, lambda flip: flip * 2 + me["x"] % 2),
    )

    def moved(axis, value):
        at = dict(me)
        at[axis] = value
        return mesh_index(at)

    def block(side, place, flip):
        ref, _, mine, _ = sides[side]
        return ref.at[place, jnp.bitwise_xor(mine, flip), core]

    def send(side, step):
        _, axis, mine, place_x = sides[side]
        here = me[axis]
        up, down = (here + 1) % RING, (here + RING - 1) % RING
        if step == 0:
            origin, flip, part, target = here, 0, None, moved("x", place_x(1 - mine))
        elif step < 5:
            flip = (step - 1) // 2
            origin, part, target = here, None, moved(axis, (up, down)[(step - 1) % 2])
        else:
            flip = (step - 5) // 2
            way = (step - 5) % 2
            origin, part, target = (down, up)[way], way * half, moved(axis, (up, down)[way])
        ref = block(side, origin, flip)
        if part is not None:
            ref = ref.at[:, pl.ds(part, half)]
        source = own_ref if side == 0 and step in (0, 1, 2) else ref
        return pltpu.make_async_remote_copy(
            src_ref=source, dst_ref=ref, send_sem=send_sem.at[side, step], recv_sem=recv_sem.at[side, step],
            device_id=target, device_id_type=MESH,
        )

    def pair(side, shift, flip):
        place = (me[sides[side][1]] + shift) % RING
        ref = block(side, place, flip)
        go = pltpu.make_async_remote_copy(
            src_ref=own_ref if side == 0 and shift == 0 and flip == 0 else ref, dst_ref=ref,
            send_sem=pair_send.at[side], recv_sem=pair_recv.at[side],
            device_id=moved("core", 1 - core), device_id_type=MESH,
        )
        if side == 0:
            go.start()
        else:
            @pl.when(place // 2 != core)
            def _():
                go.start()

    first = row_ref.at[me["z"], me["x"] % 2, core]
    local = pltpu.make_async_copy(own_ref, first, local_sem.at[0])
    local.start()
    turned = col_ref.at[chip // 2, chip % 2, core]
    turn = pltpu.make_async_remote_copy(
        src_ref=own_ref, dst_ref=turned, send_sem=turn_send, recv_sem=turn_recv,
        device_id=(chip, row * 2 + core), device_id_type=MESH,
    )
    stay = pltpu.make_async_copy(own_ref, turned, local_sem.at[1])
    at_home = row == chip

    @pl.when(at_home)
    def _():
        stay.start()

    @pl.when(jnp.logical_not(at_home))
    def _():
        turn.start()

    for step in (0, 1, 2):
        send(0, step).start()
    pair(0, 0, 0)

    @pl.when(at_home)
    def _():
        stay.wait()

    @pl.when(jnp.logical_not(at_home))
    def _():
        turn.wait_recv()

    for step in (0, 1, 2):
        send(1, step).start()
    pair(1, 0, 0)
    for side in (0, 1):
        send(side, 0).wait_recv()
        send(side, 3).start()
        send(side, 4).start()
        pair(side, 0, 1)
    for flip in (0, 1):
        for way in (0, 1):
            for side in (0, 1):
                send(side, 1 + 2 * flip + way).wait_recv()
                send(side, 5 + 2 * flip + way).start()
                pair(side, (RING - 1, 1)[way], flip)
    for flip in (0, 1):
        for side in (0, 1):
            for way in (0, 1):
                send(side, 5 + 2 * flip + way).wait_recv()
            pair(side, 2, flip)
    local.wait()

    @pl.when(jnp.logical_not(at_home))
    def _():
        turn.wait_send()

    for side in (0, 1):
        for step in range(9):
            send(side, step).wait_send()
        ref = sides[side][0].at[pl.ds(0, RING if side == 0 else 2), :, 0]
        whole = pltpu.make_async_remote_copy(
            src_ref=ref, dst_ref=ref, send_sem=pair_send.at[side], recv_sem=pair_recv.at[side],
            device_id=moved("core", 1 - core), device_id_type=MESH,
        )
        whole.wait()


def spread(rounded):
    own, size = rounded.shape
    dma = pltpu.SemaphoreType.DMA
    side = jax.ShapeDtypeStruct((RING, 2, 2, own, size), rounded.dtype)
    row_side, col_side = pl.pallas_call(
        spread_kernel,
        out_shape=(side, side),
        in_specs=[pl.BlockSpec(memory_space=VMEM)],
        out_specs=(pl.BlockSpec(memory_space=HBM),) * 2,
        scratch_shapes=[dma((2,)), dma, dma, dma((2, 9)), dma((2, 9)), dma((2,)), dma((2,))],
        compiler_params=pltpu.CompilerParams(has_side_effects=True),
        name="factor_spread",
    )(rounded)
    return row_side.reshape(16 * own, size), col_side.reshape(16 * own, size)


def finish_kernel(
    place_ref, pattern_ref, front_ref, arrived_ref, row_ref, col_ref, out_ref,
    tile, slots, rows, cols, load_sem, slot_sem, row_sem, col_sem, out_sem,
):
    total = arrived_ref.shape[0]
    chunk = slots.shape[1]
    steps = total // chunk
    bands = out_sem.shape[0]
    height, width = tile.shape[0] // bands, tile.shape[1]
    block_cols = width // SIDE
    blocks = (tile.shape[0] // SIDE) * block_cols

    def fetch(c):
        return pltpu.make_async_copy(arrived_ref.at[pl.ds(c * chunk, chunk)], slots.at[c % 2], slot_sem.at[c % 2])

    load = pltpu.make_async_copy(front_ref, tile, load_sem)
    load.start()
    fetch(0).start()
    core = lax.axis_index("col") % 2
    half = pl.ds(pl.multiple_of(core * cols.shape[0], SIDE), cols.shape[0])
    load_cols = pltpu.make_async_copy(col_ref.at[half], cols, col_sem)
    load_rows = pltpu.make_async_copy(row_ref, rows, row_sem)
    load.wait()

    for c in range(steps):
        if c + 1 < steps:
            fetch(c + 1).start()
        if c == steps - 3:
            load_cols.start()
            load_rows.start()
        fetch(c).wait()

        @pl.loop(0, chunk)
        def _(n):
            place = place_ref[c * chunk + n]

            @pl.when(place < blocks)
            def _():
                top = pl.multiple_of((place // block_cols) * SIDE, SIDE)
                left = pl.multiple_of((place % block_cols) * SIDE, SIDE)
                here = (pl.ds(top, SIDE), pl.ds(left, SIDE))
                tile[here] = tile[here] + slots[c % 2, n].astype(jnp.float32)

    load_cols.wait()
    load_rows.wait()

    def put(band):
        part = pl.ds(pl.multiple_of(band * height, height), height)
        return pltpu.make_async_copy(tile.at[part], out_ref.at[part], out_sem.at[band])

    @pl.loop(0, bands)
    def _(band):
        low = pl.multiple_of(band * height, height)
        product = lax.dot_general(
            rows[pl.ds(low, height), :], cols[...], CONTRACT_LAST, preferred_element_type=jnp.float32
        )
        for a in range(height // SIDE):
            for b in range(block_cols):
                here = (pl.ds(low + a * SIDE, SIDE), pl.ds(b * SIDE, SIDE))
                keep = pattern_ref[band * (height // SIDE) + a, b].astype(jnp.float32)
                tile[here] = tile[here] - product[a * SIDE : (a + 1) * SIDE, b * SIDE : (b + 1) * SIDE] * keep
        put(band).start()

    @pl.loop(0, bands)
    def _(band):
        put(band).wait()


def finish(places, pattern, front, arrived, row_side, col_side):
    dma = pltpu.SemaphoreType.DMA
    bands = front.shape[0] // 256
    return pl.pallas_call(
        finish_kernel,
        out_shape=jax.ShapeDtypeStruct(front.shape, front.dtype),
        grid_spec=pltpu.PrefetchScalarGridSpec(
            num_scalar_prefetch=2,
            grid=(),
            in_specs=[pl.BlockSpec(memory_space=HBM)] * 4,
            out_specs=pl.BlockSpec(memory_space=HBM),
            scratch_shapes=[
                VMEM(front.shape, jnp.float32), VMEM((2, 32, SIDE, SIDE), arrived.dtype),
                VMEM(row_side.shape, row_side.dtype), VMEM((front.shape[1], col_side.shape[1]), col_side.dtype),
                dma, dma((2,)), dma, dma, dma((bands,)),
            ],
        ),
        compiler_params=pltpu.CompilerParams(vmem_limit_bytes=62 << 20),
        name="finish",
    )(places, pattern, front, arrived, row_side, col_side)


def arrivals(dest, pos, me, blocks):
    lane = lax.broadcasted_iota(jnp.int32, dest.shape, 1)
    mine = dest == me
    first = jnp.min(jnp.where(mine, lane, dest.shape[1]), axis=1)
    last = jnp.max(jnp.where(mine, lane, -1), axis=1)
    place_first = jnp.sum(jnp.where(lane == first[:, None], pos, 0), axis=1)
    place_last = jnp.sum(jnp.where(lane == last[:, None], pos, 0), axis=1)
    place_first = jnp.where(last >= 0, place_first, blocks)
    place_last = jnp.where(last > first, place_last, blocks)
    return jnp.stack([place_first, place_last], axis=1).reshape(-1)


def per_device(front, pivot, panel, child_blocks, child_dest, child_pos, pattern):
    devices = lax.axis_size("row") * lax.axis_size("col")
    me = lax.axis_index("row") * lax.axis_size("col") + lax.axis_index("col")
    size = panel.shape[1]
    dest = child_dest[:, 0]
    outgoing = pack(dest, child_blocks, devices)
    notes = jnp.concatenate([dest[None], child_pos[None], jnp.zeros((6, dest.shape[0]), jnp.int32)], axis=0)
    everything = gather(jnp.concatenate([pivot, notes.astype(jnp.float32)], axis=1))
    outgoing, everything = lax.optimization_barrier((outgoing, everything))
    arrived = lax.all_to_all(outgoing, ("row", "col"), split_axis=0, concat_axis=0, tiled=True)
    factor, rounded = cholesky_solve(everything, panel)
    row_side, col_side = spread(rounded)
    told = everything[:, size:].reshape(devices, 8, -1).astype(jnp.int32)
    tile_blocks = (front.shape[0] // SIDE) * (front.shape[1] // SIDE)
    places = arrivals(told[:, 0], told[:, 1], me, tile_blocks)
    schur = finish(places, pattern, front, arrived, row_side, col_side)
    return (schur, factor)


def solution(mesh):
    return jax.shard_map(
        per_device,
        mesh=mesh,
        in_specs=(
            P("row", "col"),
            P(("row", "col"), None),
            P(("row", "col"), None),
            P(("row", "col"), None, None),
            P(("row", "col"), None),
            P(("row", "col")),
            P("row", "col"),
        ),
        out_specs=(P("row", "col"), P(("row", "col"), None)),
        check_vma=False,
    )
```

time: 326 us -> 212 us (0.65)
  Pallas kernels: 293 us -> 198 us
  local copies, waits for them, and re-layouts: 17.5 us -> 4.71 us
  starting transfers between devices: 11.9 us -> 5.01 us
    pallas_call x1, Pallas kernels: 125 us -> 37.1 us  [gather(): pl.pallas_call(kernel, out_shape=jax.ShapeDtypeStruct((4, 2, 4, 2, 2, row...]
    unnamed x25 -> x9, local copies, waits for them, and re-layouts: 17.1 us -> 3.71 us
    pallas_call x3 -> x2, Pallas kernels: 102 us -> 94.3 us  [the longest x1 72.9 us: spread(): pl.pallas_call(spread_kernel, out_shape=(side, side), in_specs=[pl.BlockS...]
    all_to_all x1, starting transfers between devices: 11.9 us -> 5.01 us  [per_device(): lax.all_to_all(outgoing, ('row', 'col'), split_axis=0, concat_axis=0, til...]
  transfers between devices with their start and end apart: 1 -> 1, of which waited for: 0 -> 0; matrix products, arithmetic and copies ran while one was open for 1% -> 1% of each run, Pallas kernels for 85% -> 63%
where the time goes in v2:
time: 212 us
  Pallas kernels  198 us (93%)
  starting transfers between devices  5.01 us (2%)
  local copies, waits for them, and re-layouts  4.71 us (2%)
  other arithmetic  3.51 us (2%)
    pallas_call x1, Pallas kernels, spread(): pl.pallas_call(spread_kernel, out_shape=(side, side), in_specs=[pl.BlockS...  72.9 us
    pallas_call x1, Pallas kernels, cholesky_solve(): pl.pallas_call(cholesky_kernel, out_shape=(jax.ShapeDtypeStruct((own, siz...  61.5 us
    pallas_call x1, Pallas kernels, gather(): pl.pallas_call(kernel, out_shape=jax.ShapeDtypeStruct((4, 2, 4, 2, 2, row...  37.1 us
    pallas_call x1, Pallas kernels, finish(): pl.pallas_call(finish_kernel, out_shape=jax.ShapeDtypeStruct(front.shape,...  21.4 us
    all_to_all x1, starting transfers between devices, per_device(): lax.all_to_all(outgoing, ('row', 'col'), split_axis=0, concat_axis=0, til...  5.01 us
    pallas_call x1, Pallas kernels, pack(): pl.pallas_call(pack_kernel, out_shape=jax.ShapeDtypeStruct((2 * devices,...  4.81 us
  transfers between devices with their start and end apart: 1, of which 0 were waited for; matrix products, arithmetic and copies ran while one was open for 1% of the time, Pallas kernels for 63%

profile of v2, /device:TPU:1, one launch (start us, length us, event | category | flops | bytes accessed | tf_op | source)
XLA Modules:
  0.0 211.6 jit_solution(8496820921196695161)
XLA Ops:
  0.6 0.1 pad.6.clone
  0.7 0.7 add_convert_fusion
  1.5 1.4 pad_maximum_fusion.refs_0_
  2.8 37.1 %pivot_gather.1 = f32[4,2,4,2,2,8,1152]{6,5,4,3,2,1,0:T(8,128)} custom-call(f32[8,1152]{1,0:T(8,128)} %pad_maximum_fusion.refs_0_), custom_call_target="tpu_custom_call" | custom-call | tf_op jit(solution)/shard_map/pivot_gather/pallas_call | solution.py:168
  39.9 4.8 %pack.1 = bf16[256,128,128]{2,1,0:T(8,128)(2,1)} custom-call(s32[128]{0:T(128)} %bitcast.24, bf16[128,128,128]{2,1,0:T(8,128)(2,1)} %blocks_ref.1), custom_call_target="tpu_custom_call" | custom-call | tf_op jit(solution)/shard_map/pack/pallas_call | solution.py:51
  44.7 0.0 copy-start.3
  44.7 0.0 copy-start.2
  44.8 5.0 %all-to-all-start = ((bf16[256,128,128]{2,1,0:T(8,128)(2,1)}), bf16[256,128,128]{2,1,0:T(8,128)(2,1)}, u32[]{:S(2)}, u32[]{:S(2)}) async-start(bf16[256,128,128]{2,1,0:T(8,128)(2,1)} %pack.1), calls=%async_computation | async-start | bytes 16777216 | tf_op jit(solution)/shard_map/all_to_all | solution.py:524
  49.8 0.0 copy-done.3
  49.8 0.7 copy.12.pattern_ref
  50.4 1.1 convert_bitcast_fusion
  51.5 0.1 fusion.2
  51.6 0.1 select_reduce_fusion.2
  51.7 0.2 select_reduce_fusion.1
  51.9 0.1 copy.11
  52.1 0.7 reshape.62.place_ref
  52.8 0.0 copy-done.2
  52.8 0.0 copy-start
  52.8 2.3 %copy-done = f32[4,2,4,2,2,8,1152]{6,5,4,3,2,1,0:T(8,128)S(1)} copy-done((f32[4,2,4,2,2,8,1152]{6,5,4,3,2,1,0:T(8,128)S(1)}, f32[4,2,4,2,2,8,1152]{6,5,4,3,2,1,0:T(8,128)}, u32[]{:S(2)}) %copy-start) | copy-done | bytes 4718616
  55.1 61.5 %cholesky_solve.1 = (f32[128,1024]{1,0:T(8,128)}, bf16[128,1024]{1,0:T(8,128)(2,1)S(1)}) custom-call(f32[1024,1152]{1,0:T(8,128)S(1)} %bitcast.18, f32[128,1024]{1,0:T(8,128)S(1)} %copy-done.2), custom_call_target="tpu_custom_call" | custom-call | flops 10000000000 | bytes 10000000 | tf_op jit(solution)/shard_map/cholesky_solve/pallas_call | solution.py:258
  116.6 0.0 copy-start.1
  116.6 0.7 copy-done.1
  117.3 72.9 %factor_spread.1 = (bf16[4,2,2,128,1024]{4,3,2,1,0:T(8,128)(2,1)}, bf16[4,2,2,128,1024]{4,3,2,1,0:T(8,128)(2,1)}) custom-call(bf16[128,1024]{1,0:T(8,128)(2,1)} %copy-done.1), custom_call_target="tpu_custom_call" | custom-call | tf_op jit(solution)/shard_map/factor_spread/pallas_call | solution.py:401
  190.2 0.0 all-to-all-done.arrived_ref
  190.2 21.4 %finish.1 = f32[2048,1024]{1,0:T(8,128)} custom-call(s32[256]{0:T(256)} %reshape.62.place_ref, s32[16,8]{1,0:T(8,128)} %copy.12.pattern_ref, f32[2048,1024]{1,0:T(8,128)} %front_ref.1, bf16[256,128,128]{2,1,0:T(8,128)(2,1)} %all-to-all-done.arrived_ref, bf16[2048,1024]{1,0:T(8,128)(2,1)} %bitcast.19, bf16[2048,1024]{1,0:T(8,128)(2,1)} %bitcast.20), custom_call_target="tpu_custom_call" | custom-call | tf_op jit(solution)/shard_map/finish/pallas_call | solution.py:484
  (3 shorter events, 0.0 us)
Async XLA Ops:
  44.7 5.0 %copy-start.3 = (s32[16,8]{0,1:T(8,128)S(1)}, s32[16,8]{0,1:T(8,128)}, u32[]{:S(2)}) copy-start(s32[16,8]{0,1:T(8,128)} %param.13) | copy-start | bytes 1540
  44.7 8.0 %copy-start.2 = (f32[128,1024]{1,0:T(8,128)S(1)}, f32[128,1024]{1,0:T(8,128)}, u32[]{:S(2)}) copy-start(f32[128,1024]{1,0:T(8,128)} %panel_ref.1) | copy-start | bytes 1572868
  44.8 145.4 %all-to-all-start = ((bf16[256,128,128]{2,1,0:T(8,128)(2,1)}), bf16[256,128,128]{2,1,0:T(8,128)(2,1)}, u32[]{:S(2)}, u32[]{:S(2)}) async-start(bf16[256,128,128]{2,1,0:T(8,128)(2,1)} %pack.1), calls=%async_computation | async-start | bytes 16777216 | tf_op jit(solution)/shard_map/all_to_all | solution.py:524
  52.8 2.3 %copy-start = (f32[4,2,4,2,2,8,1152]{6,5,4,3,2,1,0:T(8,128)S(1)}, f32[4,2,4,2,2,8,1152]{6,5,4,3,2,1,0:T(8,128)}, u32[]{:S(2)}) copy-start(f32[4,2,4,2,2,8,1152]{6,5,4,3,2,1,0:T(8,128)} %pivot_gather.1) | copy-start | bytes 14155780
  116.6 0.7 copy-start.1

commit v3 on v2

--- a/solution.py
+++ b/solution.py
@@ -26,6 +26,13 @@
 
 def mesh_index(at):
     return (at["y"] * 2 + at["x"] // 2, at["z"] * 4 + (at["x"] % 2) * 2 + at["core"])
+
+
+def meet(peers, more=0):
+    barrier = pltpu.get_barrier_semaphore()
+    for peer in peers:
+        pl.semaphore_signal(barrier, inc=1, device_id=peer, device_id_type=MESH)
+    pl.semaphore_wait(barrier, len(peers) + more)
 
 
 def pack_kernel(dest_ref, blocks_ref, out_ref, count, sem):
@@ -99,17 +106,19 @@
             device_id_type=MESH,
         )
 
-    def ring(piece, step):
-        done, axis = ORDERS[piece][:2], ORDERS[piece][2]
+    def ring(piece, step, turn):
+        first, axis = ORDERS[piece][1:]
         low, high = piece_bounds[piece]
         cut = low + ((high - low) // SIDE * 2 // 3) * SIDE
         up, down = (me[axis] + 1) % RING, (me[axis] + RING - 1) % RING
         origin, target, part = (
             (me[axis], up, (low, high)), (me[axis], down, (low, high)), (down, up, (low, cut)), (up, down, (cut, high)),
         )[step]
-        ref = view(piece, done, moved(axis, origin), part)
+        at = moved(axis, origin)
+        at[first] = jnp.bitwise_xor(me[first], turn)
+        ref = view(piece, ORDERS[piece][:1], at, part)
         return pltpu.make_async_remote_copy(
-            src_ref=ref, dst_ref=ref, send_sem=ring_send.at[piece, step], recv_sem=ring_recv.at[piece, step],
+            src_ref=ref, dst_ref=ref, send_sem=ring_send.at[piece, step, turn], recv_sem=ring_recv.at[piece, step, turn],
             device_id=mesh_index(moved(axis, target)), device_id_type=MESH,
         )
 
@@ -122,6 +131,8 @@
         )
 
     turns = (1, 3, 2)
+    meet([mesh_index(moved(axis, jnp.bitwise_xor(me[axis], turn))) for axis in "xyz" for turn in turns]
+         + [mesh_index(moved("core", 1 - me["core"]))])
     for piece in pieces:
         for turn in turns:
             send(piece, 0, turn).start()
@@ -131,27 +142,35 @@
             send(piece, 0, turn).wait_recv()
         for turn in turns:
             send(piece, 1, turn).start()
+        ring(piece, 0, 0).start()
+        ring(piece, 1, 0).start()
+    for turn in turns:
+        for piece in pieces:
+            send(piece, 1, turn).wait_recv()
+            ring(piece, 0, turn).start()
+            ring(piece, 1, turn).start()
     for piece in pieces:
-        for turn in turns:
-            send(piece, 1, turn).wait_recv()
-        ring(piece, 0).start()
-        ring(piece, 1).start()
         pair(piece, 0).start()
+    for turn in (0, *turns):
+        for piece in pieces:
+            for step in (0, 1):
+                ring(piece, step, turn).wait_recv()
+                ring(piece, step + 2, turn).start()
     for piece in pieces:
-        for step in (0, 1):
-            ring(piece, step).wait_recv()
-            ring(piece, step + 2).start()
-            pair(piece, step + 1).start()
+        pair(piece, 1).start()
+        pair(piece, 2).start()
     for piece in pieces:
-        ring(piece, 2).wait_recv()
-        ring(piece, 3).wait_recv()
+        for turn in (0, *turns):
+            ring(piece, 2, turn).wait_recv()
+            ring(piece, 3, turn).wait_recv()
         pair(piece, 3).start()
     for piece in pieces:
         for turn in turns:
             send(piece, 0, turn).wait_send()
             send(piece, 1, turn).wait_send()
         for step in range(4):
-            ring(piece, step).wait_send()
+            for turn in range(RING):
+                ring(piece, step, turn).wait_send()
             pair(piece, step).wait()
 
 
@@ -171,9 +190,9 @@
         in_specs=[pl.BlockSpec(memory_space=HBM)],
         out_specs=pl.BlockSpec(memory_space=HBM),
         scratch_shapes=[
-            dma, dma((count, 2, 3)), dma((count, 2, 3)), dma((count, 4)), dma((count, 4)), dma((count, 4)), dma((count, 4)),
+            dma, dma((count, 2, 3)), dma((count, 2, 3)), dma((count, 4, RING)), dma((count, 4, RING)), dma((count, 4)), dma((count, 4)),
         ],
-        compiler_params=pltpu.CompilerParams(has_side_effects=True),
+        compiler_params=pltpu.CompilerParams(has_side_effects=True, collective_id=0),
         name="pivot_gather",
     )(own)
     return out.reshape(128 * rows, width)
@@ -275,7 +294,8 @@
     me = coordinates()
     core = me["core"]
     row, chip = lax.axis_index("row"), lax.axis_index("col") // 2
-    half = own_ref.shape[1] // 2
+    parts = turn_send.shape[0]
+    width = own_ref.shape[1] // parts
     sides = (
         (row_ref, "z", me["x"] % 2, lambda flip: me["x"] // 2 * 2 + flip),
         (col_ref, "y", me["x"] // 2, lambda flip: flip * 2 + me["x"] % 2),
@@ -286,29 +306,32 @@
         at[axis] = value
         return mesh_index(at)
 
+    shifts = ((0, 0), (chip // 2, chip % 2))
+
+    def slot(side, place, flip):
+        return jnp.bitwise_xor(place, shifts[side][0]), jnp.bitwise_xor(sides[side][2], jnp.bitwise_xor(shifts[side][1], flip))
+
     def block(side, place, flip):
-        ref, _, mine, _ = sides[side]
-        return ref.at[place, jnp.bitwise_xor(mine, flip), core]
-
-    def send(side, step):
+        high, low = slot(side, place, flip)
+        return sides[side][0].at[high, low, core]
+
+    def cut(ref, q):
+        return ref.at[:, pl.ds(q * width, width)]
+
+    def send(side, kind, q):
         _, axis, mine, place_x = sides[side]
         here = me[axis]
         up, down = (here + 1) % RING, (here + RING - 1) % RING
-        if step == 0:
-            origin, flip, part, target = here, 0, None, moved("x", place_x(1 - mine))
-        elif step < 5:
-            flip = (step - 1) // 2
-            origin, part, target = here, None, moved(axis, (up, down)[(step - 1) % 2])
+        if kind == 0:
+            origin, flip, target = here, 0, moved("x", place_x(1 - mine))
+        elif kind < 5:
+            origin, flip, target = here, (kind - 1) // 2, moved(axis, (up, down)[(kind - 1) % 2])
         else:
-            flip = (step - 5) // 2
-            way = (step - 5) % 2
-            origin, part, target = (down, up)[way], way * half, moved(axis, (up, down)[way])
+            origin, flip, target = (down, up)[q % 2], kind - 5, moved(axis, (up, down)[q % 2])
         ref = block(side, origin, flip)
-        if part is not None:
-            ref = ref.at[:, pl.ds(part, half)]
-        source = own_ref if side == 0 and step in (0, 1, 2) else ref
         return pltpu.make_async_remote_copy(
-            src_ref=source, dst_ref=ref, send_sem=send_sem.at[side, step], recv_sem=recv_sem.at[side, step],
+            src_ref=cut(own_ref if side == 0 and kind < 3 else ref, q), dst_ref=cut(ref, q),
+            send_sem=send_sem.at[side, kind, q], recv_sem=recv_sem.at[side, kind, q],
             device_id=target, device_id_type=MESH,
         )
 
@@ -323,20 +346,34 @@
         if side == 0:
             go.start()
         else:
-            @pl.when(place // 2 != core)
+            @pl.when(slot(side, place, flip)[0] // 2 != core)
             def _():
                 go.start()
 
-    first = row_ref.at[me["z"], me["x"] % 2, core]
-    local = pltpu.make_async_copy(own_ref, first, local_sem.at[0])
+    turned = col_ref.at[chip // 2, chip % 2, core]
+    stay = pltpu.make_async_copy(own_ref, turned, local_sem.at[1])
+    across = (jnp.bitwise_xor(row, chip), row * 2 + core)
+    source = (chip, jnp.bitwise_xor(row, chip) * 2 + core)
+    at_home = jnp.logical_and(row == 0, chip == 0)
+
+    def turn(q):
+        return pltpu.make_async_remote_copy(
+            src_ref=cut(own_ref, q), dst_ref=cut(turned, q), send_sem=turn_send.at[q], recv_sem=turn_recv.at[q],
+            device_id=across, device_id_type=MESH,
+        )
+
+    barrier = pltpu.get_barrier_semaphore()
+
+    @pl.when(jnp.logical_not(at_home))
+    def _():
+        pl.semaphore_signal(barrier, inc=1, device_id=source, device_id_type=MESH)
+
+    peers = [moved("core", 1 - core)]
+    for _, axis, mine, place_x in sides:
+        peers += [moved(axis, (me[axis] + 1) % RING), moved(axis, (me[axis] + RING - 1) % RING), moved("x", place_x(1 - mine))]
+    meet(peers, jnp.where(at_home, 0, 1))
+    local = pltpu.make_async_copy(own_ref, row_ref.at[me["z"], me["x"] % 2, core], local_sem.at[0])
     local.start()
-    turned = col_ref.at[chip // 2, chip % 2, core]
-    turn = pltpu.make_async_remote_copy(
-        src_ref=own_ref, dst_ref=turned, send_sem=turn_send, recv_sem=turn_recv,
-        device_id=(chip, row * 2 + core), device_id_type=MESH,
-    )
-    stay = pltpu.make_async_copy(own_ref, turned, local_sem.at[1])
-    at_home = row == chip
 
     @pl.when(at_home)
     def _():
@@ -344,48 +381,57 @@
 
     @pl.when(jnp.logical_not(at_home))
     def _():
-        turn.start()
-
-    for step in (0, 1, 2):
-        send(0, step).start()
+        for q in range(parts):
+            turn(q).start()
+
+    for q in range(parts):
+        for kind in (0, 1, 2):
+            send(0, kind, q).start()
     pair(0, 0, 0)
 
     @pl.when(at_home)
     def _():
         stay.wait()
 
+    for q in range(parts):
+        @pl.when(jnp.logical_not(at_home))
+        def _():
+            turn(q).wait_recv()
+
+        for kind in (0, 1, 2):
+            send(1, kind, q).start()
+    pair(1, 0, 0)
+    for flip in (0, 1):
+        for q in range(parts):
+            for side in (0, 1):
+                if flip == 0:
+                    send(side, 0, q).wait_recv()
+                    send(side, 3, q).start()
+                    send(side, 4, q).start()
+                send(side, 1 + 2 * flip + q % 2, q).wait_recv()
+                send(side, 5 + flip, q).start()
+    for flip in (0, 1):
+        for side in (0, 1):
+            if flip == 0:
+                pair(side, 0, 1)
+            for q in range(parts):
+                send(side, 2 + 2 * flip - q % 2, q).wait_recv()
+            pair(side, RING - 1, flip)
+            pair(side, 1, flip)
+            for q in range(parts):
+                send(side, 5 + flip, q).wait_recv()
+            pair(side, 2, flip)
+    local.wait()
+
     @pl.when(jnp.logical_not(at_home))
     def _():
-        turn.wait_recv()
-
-    for step in (0, 1, 2):
-        send(1, step).start()
-    pair(1, 0, 0)
+        for q in range(parts):
+            turn(q).wait_send()
+
     for side in (0, 1):
-        send(side, 0).wait_recv()
-        send(side, 3).start()
-        send(side, 4).start()
-        pair(side, 0, 1)
-    for flip in (0, 1):
-        for way in (0, 1):
-            for side in (0, 1):
-                send(side, 1 + 2 * flip + way).wait_recv()
-                send(side, 5 + 2 * flip + way).start()
-                pair(side, (RING - 1, 1)[way], flip)
-    for flip in (0, 1):
-        for side in (0, 1):
-            for way in (0, 1):
-                send(side, 5 + 2 * flip + way).wait_recv()
-            pair(side, 2, flip)
-    local.wait()
-
-    @pl.when(jnp.logical_not(at_home))
-    def _():
-        turn.wait_send()
-
-    for side in (0, 1):
-        for step in range(9):
-            send(side, step).wait_send()
+        for kind in range(7):
+            for q in range(parts):
+                send(side, kind, q).wait_send()
         ref = sides[side][0].at[pl.ds(0, RING if side == 0 else 2), :, 0]
         whole = pltpu.make_async_remote_copy(
             src_ref=ref, dst_ref=ref, send_sem=pair_send.at[side], recv_sem=pair_recv.at[side],
@@ -398,109 +444,136 @@
     own, size = rounded.shape
     dma = pltpu.SemaphoreType.DMA
     side = jax.ShapeDtypeStruct((RING, 2, 2, own, size), rounded.dtype)
+    parts = 4
     row_side, col_side = pl.pallas_call(
         spread_kernel,
         out_shape=(side, side),
         in_specs=[pl.BlockSpec(memory_space=VMEM)],
-        out_specs=(pl.BlockSpec(memory_space=HBM),) * 2,
-        scratch_shapes=[dma((2,)), dma, dma, dma((2, 9)), dma((2, 9)), dma((2,)), dma((2,))],
-        compiler_params=pltpu.CompilerParams(has_side_effects=True),
+        out_specs=(pl.BlockSpec(memory_space=SPREAD_SPACE),) * 2,
+        scratch_shapes=[
+            dma((2,)), dma((parts,)), dma((parts,)), dma((2, 7, parts)), dma((2, 7, parts)), dma((2,)), dma((2,)),
+        ],
+        compiler_params=pltpu.CompilerParams(has_side_effects=True, collective_id=1, vmem_limit_bytes=SPREAD_LIMIT),
         name="factor_spread",
     )(rounded)
     return row_side.reshape(16 * own, size), col_side.reshape(16 * own, size)
 
 
+SPREAD_SPACE = HBM
+SPREAD_LIMIT = 62 << 20
+
+
+UNROLL = 4
+
+
 def finish_kernel(
-    place_ref, pattern_ref, front_ref, arrived_ref, row_ref, col_ref, out_ref,
-    tile, slots, rows, cols, load_sem, slot_sem, row_sem, col_sem, out_sem,
+    slot_ref, place_ref, start_ref, pattern_ref, front_ref, arrived_ref, row_ref, col_ref, out_ref,
+    tile, product, slots, rows, cols, front_sem, slot_sem, row_sem, col_sem, out_sem,
 ):
-    total = arrived_ref.shape[0]
-    chunk = slots.shape[1]
-    steps = total // chunk
     bands = out_sem.shape[0]
-    height, width = tile.shape[0] // bands, tile.shape[1]
+    full, width = product.shape
+    height = full // bands
+    chunk = slots.shape[0] // bands
     block_cols = width // SIDE
-    blocks = (tile.shape[0] // SIDE) * block_cols
-
-    def fetch(c):
-        return pltpu.make_async_copy(arrived_ref.at[pl.ds(c * chunk, chunk)], slots.at[c % 2], slot_sem.at[c % 2])
-
-    load = pltpu.make_async_copy(front_ref, tile, load_sem)
-    load.start()
-    fetch(0).start()
+    blocks = (full // SIDE) * block_cols
     core = lax.axis_index("col") % 2
-    half = pl.ds(pl.multiple_of(core * cols.shape[0], SIDE), cols.shape[0])
+
+    def band(b):
+        return pl.ds(pl.multiple_of(b * height, height), height)
+
+    def part(b):
+        return pl.ds(b * chunk, chunk)
+
+    half = pl.ds(pl.multiple_of(core * width, SIDE), width)
     load_cols = pltpu.make_async_copy(col_ref.at[half], cols, col_sem)
-    load_rows = pltpu.make_async_copy(row_ref, rows, row_sem)
-    load.wait()
-
-    for c in range(steps):
-        if c + 1 < steps:
-            fetch(c + 1).start()
-        if c == steps - 3:
-            load_cols.start()
-            load_rows.start()
-        fetch(c).wait()
-
-        @pl.loop(0, chunk)
-        def _(n):
-            place = place_ref[c * chunk + n]
-
-            @pl.when(place < blocks)
-            def _():
+
+    def load_front(b):
+        return pltpu.make_async_copy(front_ref.at[band(b)], tile.at[band(b)], front_sem.at[b])
+
+    def load_rows(b):
+        return pltpu.make_async_copy(row_ref.at[band(b)], rows.at[band(b)], row_sem.at[b])
+
+    def load_slots(b):
+        return pltpu.make_async_copy(arrived_ref.at[part(b)], slots.at[part(b)], slot_sem.at[b])
+
+    def put(b):
+        return pltpu.make_async_copy(tile.at[band(b)], out_ref.at[band(b)], out_sem.at[b])
+
+    load_cols.start()
+    for b in range(bands):
+        load_rows(b).start()
+    load_cols.wait()
+    for b in range(bands):
+        load_rows(b).wait()
+    for load in (load_slots, load_front):
+        for b in range(bands):
+            load(b).start()
+
+    @pl.loop(0, bands)
+    def _(b):
+        value = lax.dot_general(rows[band(b), :], cols[...], CONTRACT_LAST, preferred_element_type=jnp.float32)
+        for i in range(height // SIDE):
+            for j in range(block_cols):
+                keep = pattern_ref[b * (height // SIDE) + i, j].astype(jnp.float32)
+                here = (pl.ds(pl.multiple_of(b * height + i * SIDE, SIDE), SIDE), pl.ds(j * SIDE, SIDE))
+                product[here] = value[i * SIDE : (i + 1) * SIDE, j * SIDE : (j + 1) * SIDE] * keep
+
+    for b in range(bands):
+        load_slots(b).wait()
+
+    @pl.loop(0, bands)
+    def _(b):
+        load_front(b).wait()
+        low, high = start_ref[b], start_ref[b + 1]
+
+        @pl.loop(0, (high - low + UNROLL - 1) // UNROLL)
+        def _(t):
+            for n in range(UNROLL):
+                entry = low + t * UNROLL + n
+                place = jnp.where(entry < high, place_ref[entry], blocks)
                 top = pl.multiple_of((place // block_cols) * SIDE, SIDE)
                 left = pl.multiple_of((place % block_cols) * SIDE, SIDE)
                 here = (pl.ds(top, SIDE), pl.ds(left, SIDE))
-                tile[here] = tile[here] + slots[c % 2, n].astype(jnp.float32)
-
-    load_cols.wait()
-    load_rows.wait()
-
-    def put(band):
-        part = pl.ds(pl.multiple_of(band * height, height), height)
-        return pltpu.make_async_copy(tile.at[part], out_ref.at[part], out_sem.at[band])
+                tile[here] = tile[here] + slots[slot_ref[entry]].astype(jnp.float32)
+
+        tile[band(b), :] = tile[band(b), :] - product[band(b), :]
+        put(b).start()
 
     @pl.loop(0, bands)
-    def _(band):
-        low = pl.multiple_of(band * height, height)
-        product = lax.dot_general(
-            rows[pl.ds(low, height), :], cols[...], CONTRACT_LAST, preferred_element_type=jnp.float32
-        )
-        for a in range(height // SIDE):
-            for b in range(block_cols):
-                here = (pl.ds(low + a * SIDE, SIDE), pl.ds(b * SIDE, SIDE))
-                keep = pattern_ref[band * (height // SIDE) + a, b].astype(jnp.float32)
-                tile[here] = tile[here] - product[a * SIDE : (a + 1) * SIDE, b * SIDE : (b + 1) * SIDE] * keep
-        put(band).start()
-
-    @pl.loop(0, bands)
-    def _(band):
-        put(band).wait()
-
-
-def finish(places, pattern, front, arrived, row_side, col_side):
+    def _(b):
+        put(b).wait()
+
+
+def finish(plan, pattern, front, arrived, row_side, col_side):
     dma = pltpu.SemaphoreType.DMA
-    bands = front.shape[0] // 256
+    height, width = front.shape
+    size = row_side.shape[1]
+    bands = height // BAND
     return pl.pallas_call(
         finish_kernel,
         out_shape=jax.ShapeDtypeStruct(front.shape, front.dtype),
         grid_spec=pltpu.PrefetchScalarGridSpec(
-            num_scalar_prefetch=2,
+            num_scalar_prefetch=4,
             grid=(),
             in_specs=[pl.BlockSpec(memory_space=HBM)] * 4,
             out_specs=pl.BlockSpec(memory_space=HBM),
             scratch_shapes=[
-                VMEM(front.shape, jnp.float32), VMEM((2, 32, SIDE, SIDE), arrived.dtype),
-                VMEM(row_side.shape, row_side.dtype), VMEM((front.shape[1], col_side.shape[1]), col_side.dtype),
-                dma, dma((2,)), dma, dma, dma((bands,)),
+                VMEM((height + SIDE, width), jnp.float32), VMEM(front.shape, jnp.float32),
+                VMEM(arrived.shape, arrived.dtype), VMEM(row_side.shape, row_side.dtype), VMEM((width, size), col_side.dtype),
+                dma((bands,)), dma((bands,)), dma((bands,)), dma, dma((bands,)),
             ],
         ),
         compiler_params=pltpu.CompilerParams(vmem_limit_bytes=62 << 20),
         name="finish",
-    )(places, pattern, front, arrived, row_side, col_side)
-
-
-def arrivals(dest, pos, me, blocks):
+    )(*plan, pattern, front, arrived, row_side, col_side)
+
+
+BAND = 256
+
+
+def arrivals(dest, pos, me, tile_rows, tile_cols):
+    block_cols = tile_cols // SIDE
+    blocks = (tile_rows // SIDE) * block_cols
     lane = lax.broadcasted_iota(jnp.int32, dest.shape, 1)
     mine = dest == me
     first = jnp.min(jnp.where(mine, lane, dest.shape[1]), axis=1)
@@ -509,7 +582,18 @@
     place_last = jnp.sum(jnp.where(lane == last[:, None], pos, 0), axis=1)
     place_first = jnp.where(last >= 0, place_first, blocks)
     place_last = jnp.where(last > first, place_last, blocks)
-    return jnp.stack([place_first, place_last], axis=1).reshape(-1)
+    count = dest.shape[0]
+    number = jnp.arange(count, dtype=jnp.int32)
+    place = jnp.concatenate([place_first, place_last])
+    key = place * (2 * count) + jnp.concatenate([2 * number, 2 * number + 1])
+    rank = jnp.sum((key[:, None] > key[None, :]).astype(jnp.int32), axis=1)
+    at = rank[None, :] == jnp.arange(2 * count, dtype=jnp.int32)[:, None]
+    ordered = jnp.sum(jnp.where(at, key[None, :], 0), axis=1)
+    edges = jnp.arange(tile_rows // BAND + 1, dtype=jnp.int32) * (BAND // SIDE * block_cols)
+    starts = jnp.sum((place[None, :] < edges[:, None]).astype(jnp.int32), axis=1)
+    spare = jnp.full((UNROLL,), blocks * 2 * count, jnp.int32)
+    ordered = jnp.concatenate([ordered, spare])
+    return ordered % (2 * count), ordered // (2 * count), starts
 
 
 def per_device(front, pivot, panel, child_blocks, child_dest, child_pos, pattern):
@@ -522,12 +606,12 @@
     everything = gather(jnp.concatenate([pivot, notes.astype(jnp.float32)], axis=1))
     outgoing, everything = lax.optimization_barrier((outgoing, everything))
     arrived = lax.all_to_all(outgoing, ("row", "col"), split_axis=0, concat_axis=0, tiled=True)
+    told = everything[:, size:].reshape(devices, 8, -1).astype(jnp.int32)
+    plan = arrivals(told[:, 0], told[:, 1], me, *front.shape)
+    panel, plan, pattern = lax.optimization_barrier((panel, plan, pattern))
     factor, rounded = cholesky_solve(everything, panel)
     row_side, col_side = spread(rounded)
-    told = everything[:, size:].reshape(devices, 8, -1).astype(jnp.int32)
-    tile_blocks = (front.shape[0] // SIDE) * (front.shape[1] // SIDE)
-    places = arrivals(told[:, 0], told[:, 1], me, tile_blocks)
-    schur = finish(places, pattern, front, arrived, row_side, col_side)
+    schur = finish(plan, pattern, front, arrived, row_side, col_side)
     return (schur, factor)
 
 

time: 212 us -> 191 us (0.901); the launches traced: 212 us -> 188 us
  Pallas kernels: 198 us -> 173 us
    pallas_call x1, Pallas kernels: 72.9 us -> 63.3 us  [spread(): pl.pallas_call(spread_kernel, out_shape=(side, side), in_specs=[pl.BlockS...]
    pallas_call x1, Pallas kernels: 21.4 us -> 13.9 us  [finish(): pl.pallas_call(finish_kernel, out_shape=jax.ShapeDtypeStruct(front.shape,...]
    pallas_call x1, Pallas kernels: 37.1 us -> 29.6 us  [gather(): pl.pallas_call(kernel, out_shape=jax.ShapeDtypeStruct((4, 2, 4, 2, 2, row...]
  transfers between devices with their start and end apart: 1 -> 1, of which waited for: 0 -> 0; matrix products, arithmetic and copies ran while one was open for 1% -> 2% of each run, Pallas kernels for 63% -> 66%
where the time goes in v3:
time: 191 us; the launch traced here: 188 us
  Pallas kernels  173 us (91%)
  starting transfers between devices  5.42 us (3%)
  other arithmetic  5.09 us (3%)
  local copies, waits for them, and re-layouts  3.87 us (2%)
    pallas_call x1, Pallas kernels, spread(): pl.pallas_call(spread_kernel, out_shape=(side, side), in_specs=[pl.BlockS...  63.3 us
    pallas_call x1, Pallas kernels, cholesky_solve(): pl.pallas_call(cholesky_kernel, out_shape=(jax.ShapeDtypeStruct((own, siz...  61.5 us
    pallas_call x1, Pallas kernels, gather(): pl.pallas_call(kernel, out_shape=jax.ShapeDtypeStruct((4, 2, 4, 2, 2, row...  29.6 us
    pallas_call x1, Pallas kernels, finish(): pl.pallas_call(finish_kernel, out_shape=jax.ShapeDtypeStruct(front.shape,...  13.9 us
    all_to_all x1, starting transfers between devices, per_device(): lax.all_to_all(outgoing, ('row', 'col'), split_axis=0, concat_axis=0, til...  5.42 us
    pallas_call x1, Pallas kernels, pack(): pl.pallas_call(pack_kernel, out_shape=jax.ShapeDtypeStruct((2 * devices,...  4.81 us
  transfers between devices with their start and end apart: 1, of which 0 were waited for; matrix products, arithmetic and copies ran while one was open for 2% of the time, Pallas kernels for 66%

profile of v3, /device:TPU:1, one launch (start us, length us, event | category | flops | bytes accessed | tf_op | source)
XLA Modules:
  0.0 188.2 jit_solution(13264394900233096404)
XLA Ops:
  0.6 0.1 pad.9.clone
  0.7 0.7 add_convert_fusion
  1.5 1.4 pad_maximum_fusion.refs_0_
  2.8 29.6 %pivot_gather.1 = f32[4,2,4,2,2,8,1152]{6,5,4,3,2,1,0:T(8,128)} custom-call(f32[8,1152]{1,0:T(8,128)} %pad_maximum_fusion.refs_0_), custom_call_target="tpu_custom_call" | custom-call | tf_op jit(solution)/shard_map/pivot_gather/pallas_call | solution.py:187
  32.4 4.8 %pack.1 = bf16[256,128,128]{2,1,0:T(8,128)(2,1)} custom-call(s32[128]{0:T(128)} %bitcast.20, bf16[128,128,128]{2,1,0:T(8,128)(2,1)} %blocks_ref.1), custom_call_target="tpu_custom_call" | custom-call | tf_op jit(solution)/shard_map/pack/pallas_call | solution.py:58
  37.2 0.0 copy-start.3
  37.2 0.0 copy-start.2
  37.2 5.4 %all-to-all-start = ((bf16[256,128,128]{2,1,0:T(8,128)(2,1)}), bf16[256,128,128]{2,1,0:T(8,128)(2,1)}, u32[]{:S(2)}, u32[]{:S(2)}) async-start(bf16[256,128,128]{2,1,0:T(8,128)(2,1)} %pack.1), calls=%async_computation | async-start | bytes 16777216 | tf_op jit(solution)/shard_map/all_to_all | solution.py:608
  42.7 1.1 convert_bitcast_fusion
  43.8 0.1 fusion.2
  43.9 0.1 select_reduce_fusion.3
  44.0 0.2 select_reduce_fusion.2
  44.2 0.2 convert_reduce_fusion
  44.4 0.1 select_reduce_fusion
  44.5 0.6 add_select_fusion
  45.1 0.7 convert_reduce_fusion.1.start_ref
  45.8 0.0 copy-done.3
  45.8 0.7 copy.13.pattern_ref
  46.4 0.0 copy-done.2
  46.4 0.0 copy-start
  46.4 2.3 %copy-done = f32[4,2,4,2,2,8,1152]{6,5,4,3,2,1,0:T(8,128)S(1)} copy-done((f32[4,2,4,2,2,8,1152]{6,5,4,3,2,1,0:T(8,128)S(1)}, f32[4,2,4,2,2,8,1152]{6,5,4,3,2,1,0:T(8,128)}, u32[]{:S(2)}) %copy-start) | copy-done | bytes 4718616
  48.8 61.5 %cholesky_solve.1 = (f32[128,1024]{1,0:T(8,128)}, bf16[128,1024]{1,0:T(8,128)(2,1)S(1)}) custom-call(f32[1024,1152]{1,0:T(8,128)S(1)} %bitcast.14, f32[128,1024]{1,0:T(8,128)S(1)} %copy-done.2), custom_call_target="tpu_custom_call" | custom-call | flops 10000000000 | bytes 10000000 | tf_op jit(solution)/shard_map/cholesky_solve/pallas_call | solution.py:277
  110.2 0.0 copy-start.1
  110.2 0.7 copy-done.1
  110.9 63.3 %factor_spread.1 = (bf16[4,2,2,128,1024]{4,3,2,1,0:T(8,128)(2,1)}, bf16[4,2,2,128,1024]{4,3,2,1,0:T(8,128)(2,1)}) custom-call(bf16[128,1024]{1,0:T(8,128)(2,1)} %copy-done.1), custom_call_target="tpu_custom_call" | custom-call | tf_op jit(solution)/shard_map/factor_spread/pallas_call | solution.py:448
  174.3 0.0 all-to-all-done.arrived_ref
  174.3 13.9 %finish.1 = f32[2048,1024]{1,0:T(8,128)} custom-call(s32[260]{0:T(512)} %get-tuple-element.14.slot_ref, s32[260]{0:T(512)} %get-tuple-element.15.place_ref, s32[9]{0:T(128)} %convert_reduce_fusion.1.start_ref, s32[16,8]{1,0:T(8,128)} %copy.13.pattern_ref, f32[2048,1024]{1,0:T(8,128)} %front_ref.1, bf16[256,128,128]{2,1,0:T(8,128)(2,1)} %all-to-all-done.arrived_ref, ...), custom_call_target="tpu_custom_call" | custom-call | tf_op jit(solution)/shard_map/finish/pallas_call | solution.py:552
  (5 shorter events, 0.0 us)
Async XLA Ops:
  37.2 8.6 %copy-start.3 = (s32[16,8]{0,1:T(8,128)S(1)}, s32[16,8]{0,1:T(8,128)}, u32[]{:S(2)}) copy-start(s32[16,8]{0,1:T(8,128)} %param.13) | copy-start | bytes 1540
  37.2 9.2 %copy-start.2 = (f32[128,1024]{1,0:T(8,128)S(1)}, f32[128,1024]{1,0:T(8,128)}, u32[]{:S(2)}) copy-start(f32[128,1024]{1,0:T(8,128)} %panel_ref) | copy-start | bytes 1572868
  37.2 137.1 %all-to-all-start = ((bf16[256,128,128]{2,1,0:T(8,128)(2,1)}), bf16[256,128,128]{2,1,0:T(8,128)(2,1)}, u32[]{:S(2)}, u32[]{:S(2)}) async-start(bf16[256,128,128]{2,1,0:T(8,128)(2,1)} %pack.1), calls=%async_computation | async-start | bytes 16777216 | tf_op jit(solution)/shard_map/all_to_all | solution.py:608
  46.4 2.3 %copy-start = (f32[4,2,4,2,2,8,1152]{6,5,4,3,2,1,0:T(8,128)S(1)}, f32[4,2,4,2,2,8,1152]{6,5,4,3,2,1,0:T(8,128)}, u32[]{:S(2)}) copy-start(f32[4,2,4,2,2,8,1152]{6,5,4,3,2,1,0:T(8,128)} %pivot_gather.1) | copy-start | bytes 14155780
  110.2 0.7 copy-start.1

commit v4 on v3

--- a/solution.py
+++ b/solution.py
@@ -35,108 +35,125 @@
     pl.semaphore_wait(barrier, len(peers) + more)
 
 
-def pack_kernel(dest_ref, blocks_ref, out_ref, count, sem):
+def pack_kernel(dest_ref, blocks_ref, out_ref, blocks, count, load_sem, sem):
     devices = count.shape[0]
-    number = blocks_ref.shape[0]
+    chunks = load_sem.shape[0]
+    chunk = blocks.shape[0] // chunks
+
+    def load(c):
+        part = pl.ds(c * chunk, chunk)
+        return pltpu.make_async_copy(blocks_ref.at[part], blocks.at[part], load_sem.at[c])
+
+    for c in range(chunks):
+        load(c).start()
 
     @pl.loop(0, devices)
     def _(d):
         count[d] = 0
 
-    @pl.loop(0, number)
-    def _(i):
-        owner = dest_ref[i]
-        used = count[owner]
-        count[owner] = used + 1
-        pltpu.make_async_copy(blocks_ref.at[i], out_ref.at[owner * 2 + used], sem).start()
-
-    pltpu.make_async_copy(blocks_ref, blocks_ref, sem).wait()
+    for c in range(chunks):
+        load(c).wait()
+
+        @pl.loop(c * chunk, (c + 1) * chunk)
+        def _(i):
+            owner = dest_ref[i]
+            used = count[owner]
+            count[owner] = used + 1
+            pltpu.make_async_copy(blocks.at[i], out_ref.at[owner * 2 + used], sem).start()
+
+    pltpu.make_async_copy(blocks, blocks, sem).wait()
 
 
 def pack(dest, blocks, devices):
     number, side, _ = blocks.shape
+    dma = pltpu.SemaphoreType.DMA
     return pl.pallas_call(
         pack_kernel,
         out_shape=jax.ShapeDtypeStruct((2 * devices, side, side), blocks.dtype),
         grid_spec=pltpu.PrefetchScalarGridSpec(
             num_scalar_prefetch=1,
             grid=(),
-            in_specs=[pl.BlockSpec(memory_space=VMEM)],
+            in_specs=[pl.BlockSpec(memory_space=HBM)],
             out_specs=pl.BlockSpec(memory_space=HBM),
-            scratch_shapes=[pltpu.SMEM((devices,), jnp.int32), pltpu.SemaphoreType.DMA],
+            scratch_shapes=[VMEM(blocks.shape, blocks.dtype), pltpu.SMEM((devices,), jnp.int32), dma((4,)), dma],
         ),
+        compiler_params=pltpu.CompilerParams(vmem_limit_bytes=62 << 20),
         name="pack",
     )(dest, blocks)
 
 
 ORDERS = (("x", "y", "z"), ("y", "z", "x"), ("z", "x", "y"))
 RING = 4
-
-
-def gather_kernel(piece_bounds, own_ref, out_ref, local_sem, send_sem, recv_sem, ring_send, ring_recv, pair_send, pair_recv):
+NOTED = 128
+
+
+def gather_kernel(pivot_ref, notes_ref, *refs):
+    outs, (local_sem, send_sem, recv_sem, ring_send, ring_recv, pair_send, pair_recv) = refs[:3], refs[3:]
     me = coordinates()
     pieces = range(len(ORDERS))
-
-    def view(piece, done, at, part=None):
-        low, high = piece_bounds[piece] if part is None else part
-        pick = lambda value, axis: slice(None) if axis in done else value
-        return out_ref.at[
-            pick(at["y"], "y"), pick(at["x"] // 2, "x"), pick(at["z"], "z"), pick(at["x"] % 2, "x"), me["core"],
-            :, pl.ds(low, high - low),
-        ]
+    width = outs[0].shape[-1]
+    rest = pivot_ref.shape[1] - 2 * width
+    core = me["core"]
 
     def moved(axis, value):
         at = dict(me)
         at[axis] = value
         return at
 
-    copy = pltpu.make_async_copy(own_ref, out_ref.at[me["y"], me["x"] // 2, me["z"], me["x"] % 2, me["core"]], local_sem)
-    copy.start()
+    def places(piece):
+        return tuple(me[axis] for axis in ORDERS[piece])
 
     def send(piece, stage, turn):
-        done, axis = ORDERS[piece][:stage], ORDERS[piece][stage]
-        low, high = piece_bounds[piece]
-        there = view(piece, done, me)
+        first, second, last = places(piece)
+        axis = ORDERS[piece][stage]
+        ref = outs[piece].at[core, last, second, first] if stage == 0 else outs[piece].at[core, last, second]
         return pltpu.make_async_remote_copy(
-            src_ref=own_ref.at[:, pl.ds(low, high - low)] if stage == 0 else there,
-            dst_ref=there,
-            send_sem=send_sem.at[piece, stage, turn - 1],
-            recv_sem=recv_sem.at[piece, stage, turn - 1],
-            device_id=mesh_index(moved(axis, jnp.bitwise_xor(me[axis], turn))),
-            device_id_type=MESH,
+            src_ref=ref, dst_ref=ref,
+            send_sem=send_sem.at[piece, stage, turn - 1], recv_sem=recv_sem.at[piece, stage, turn - 1],
+            device_id=mesh_index(moved(axis, jnp.bitwise_xor(me[axis], turn))), device_id_type=MESH,
         )
 
     def ring(piece, step, turn):
-        first, axis = ORDERS[piece][1:]
-        low, high = piece_bounds[piece]
-        cut = low + ((high - low) // SIDE * 2 // 3) * SIDE
-        up, down = (me[axis] + 1) % RING, (me[axis] + RING - 1) % RING
-        origin, target, part = (
-            (me[axis], up, (low, high)), (me[axis], down, (low, high)), (down, up, (low, cut)), (up, down, (cut, high)),
-        )[step]
-        at = moved(axis, origin)
-        at[first] = jnp.bitwise_xor(me[first], turn)
-        ref = view(piece, ORDERS[piece][:1], at, part)
+        _, second, last = places(piece)
+        axis = ORDERS[piece][2]
+        up, down = (last + 1) % RING, (last + RING - 1) % RING
+        origin, target = ((last, up), (last, down), (down, up), (up, down))[step]
+        ref = outs[piece].at[core, origin, jnp.bitwise_xor(second, turn)]
+        if step >= 2:
+            ref = ref.at[pl.ds((step - 2) * 2, 2)]
         return pltpu.make_async_remote_copy(
             src_ref=ref, dst_ref=ref, send_sem=ring_send.at[piece, step, turn], recv_sem=ring_recv.at[piece, step, turn],
             device_id=mesh_index(moved(axis, target)), device_id_type=MESH,
         )
 
     def pair(piece, step):
-        done, axis = ORDERS[piece][:2], ORDERS[piece][2]
-        ref = view(piece, done, moved(axis, (me[axis] + (0, RING - 1, 1, 2)[step]) % RING))
+        last = places(piece)[2]
+        ref = outs[piece].at[core, (last + (0, RING - 1, 1, 2)[step]) % RING]
         return pltpu.make_async_remote_copy(
             src_ref=ref, dst_ref=ref, send_sem=pair_send.at[piece, step], recv_sem=pair_recv.at[piece, step],
-            device_id=mesh_index(moved("core", 1 - me["core"])), device_id_type=MESH,
-        )
-
+            device_id=mesh_index(moved("core", 1 - core)), device_id_type=MESH,
+        )
+
+    def own(piece):
+        first, second, last = places(piece)
+        return outs[piece].at[core, last, second, first]
+
+    copies = (
+        pltpu.make_async_copy(pivot_ref.at[:, pl.ds(0, width)], own(0), local_sem.at[0]),
+        pltpu.make_async_copy(pivot_ref.at[:, pl.ds(width, width)], own(1), local_sem.at[1]),
+        pltpu.make_async_copy(pivot_ref.at[:, pl.ds(2 * width, rest)], own(2).at[:, pl.ds(0, rest)], local_sem.at[2]),
+        pltpu.make_async_copy(notes_ref, own(2).at[:, pl.ds(rest, NOTED)], local_sem.at[3]),
+    )
+    for copy in copies:
+        copy.start()
     turns = (1, 3, 2)
     meet([mesh_index(moved(axis, jnp.bitwise_xor(me[axis], turn))) for axis in "xyz" for turn in turns]
-         + [mesh_index(moved("core", 1 - me["core"]))])
+         + [mesh_index(moved("core", 1 - core))])
+    for copy in copies:
+        copy.wait()
     for piece in pieces:
         for turn in turns:
             send(piece, 0, turn).start()
-    copy.wait()
     for piece in pieces:
         for turn in turns:
             send(piece, 0, turn).wait_recv()
@@ -174,28 +191,21 @@
             pair(piece, step).wait()
 
 
-def gather(own):
-    rows, width = own.shape
-    third = (width // SIDE // 3) * SIDE
-    bounds = ((0, third), (third, 2 * third), (2 * third, width))
+def gather(pivot, notes):
+    rows, width = pivot.shape[0], (pivot.shape[1] + NOTED) // 3
     count = len(ORDERS)
     dma = pltpu.SemaphoreType.DMA
-
-    def kernel(*refs):
-        gather_kernel(bounds, *refs)
-
-    out = pl.pallas_call(
-        kernel,
-        out_shape=jax.ShapeDtypeStruct((4, 2, 4, 2, 2, rows, width), own.dtype),
-        in_specs=[pl.BlockSpec(memory_space=HBM)],
-        out_specs=pl.BlockSpec(memory_space=HBM),
+    return pl.pallas_call(
+        gather_kernel,
+        out_shape=(jax.ShapeDtypeStruct((2, RING, RING, RING, rows, width), pivot.dtype),) * 3,
+        in_specs=[pl.BlockSpec(memory_space=VMEM)] * 2,
+        out_specs=(pl.BlockSpec(memory_space=HBM),) * 3,
         scratch_shapes=[
-            dma, dma((count, 2, 3)), dma((count, 2, 3)), dma((count, 4, RING)), dma((count, 4, RING)), dma((count, 4)), dma((count, 4)),
+            dma((4,)), dma((count, 2, 3)), dma((count, 2, 3)), dma((count, 4, RING)), dma((count, 4, RING)), dma((count, 4)), dma((count, 4)),
         ],
-        compiler_params=pltpu.CompilerParams(has_side_effects=True, collective_id=0),
+        compiler_params=pltpu.CompilerParams(has_side_effects=True, collective_id=0, vmem_limit_bytes=62 << 20),
         name="pivot_gather",
-    )(own)
-    return out.reshape(128 * rows, width)
+    )(pivot, notes)
 
 
 def factor_block(load, store):
@@ -237,11 +247,22 @@
             store(SUB * g + j, w[0:1, :])
 
 
-def cholesky_kernel(pivot_ref, panel_ref, factor_ref, rounded_ref, work, solved, inverse):
+def cholesky_kernel(left_ref, middle_ref, right_ref, panel_ref, factor_ref, rounded_ref, work, solved, inverse):
     size = factor_ref.shape[1]
     own = panel_ref.shape[0]
     blocks = size // SIDE
-    work[pl.ds(0, size), :] = pivot_ref[:, pl.ds(0, size)]
+
+    @pl.loop(0, size // SUB)
+    def _(d):
+        row, col = d // 16, d % 16
+        at = {"y": row // 2, "x": (row % 2) * 2 + (col // 2) % 2, "z": col // 4}
+        here = pl.ds(pl.multiple_of(d * SUB, SUB), SUB)
+        for piece, ref in enumerate((left_ref, middle_ref, right_ref)):
+            first, second, last = (at[axis] for axis in ORDERS[piece])
+            low = piece * ref.shape[-1]
+            keep = min(ref.shape[-1], size - low)
+            work[here, pl.ds(low, keep)] = ref[col % 2, last, second, first, :, pl.ds(0, keep)]
+
     work[pl.ds(size, own), :] = panel_ref[...]
 
     @pl.loop(0, blocks)
@@ -272,12 +293,12 @@
             )
 
 
-def cholesky_solve(pivot, panel):
+def cholesky_solve(pieces, panel):
     own, size = panel.shape
     return pl.pallas_call(
         cholesky_kernel,
         out_shape=(jax.ShapeDtypeStruct((own, size), jnp.float32), jax.ShapeDtypeStruct((own, size), jnp.bfloat16)),
-        in_specs=[pl.BlockSpec(memory_space=VMEM)] * 2,
+        in_specs=[pl.BlockSpec(memory_space=VMEM)] * 4,
         out_specs=(pl.BlockSpec(memory_space=VMEM),) * 2,
         scratch_shapes=[
             VMEM((size + own, size), jnp.float32), VMEM((size + own, SIDE), jnp.float32), VMEM((SIDE, SIDE), jnp.float32),
@@ -285,7 +306,7 @@
         compiler_params=pltpu.CompilerParams(vmem_limit_bytes=30 << 20),
         cost_estimate=pl.CostEstimate(flops=10**10, bytes_accessed=10**7, transcendentals=0),
         name="cholesky_solve",
-    )(pivot, panel)
+    )(*pieces, panel)
 
 
 def spread_kernel(
@@ -599,15 +620,15 @@
 def per_device(front, pivot, panel, child_blocks, child_dest, child_pos, pattern):
     devices = lax.axis_size("row") * lax.axis_size("col")
     me = lax.axis_index("row") * lax.axis_size("col") + lax.axis_index("col")
-    size = panel.shape[1]
     dest = child_dest[:, 0]
     outgoing = pack(dest, child_blocks, devices)
     notes = jnp.concatenate([dest[None], child_pos[None], jnp.zeros((6, dest.shape[0]), jnp.int32)], axis=0)
-    everything = gather(jnp.concatenate([pivot, notes.astype(jnp.float32)], axis=1))
+    everything = gather(pivot, notes.astype(jnp.float32))
     outgoing, everything = lax.optimization_barrier((outgoing, everything))
     arrived = lax.all_to_all(outgoing, ("row", "col"), split_axis=0, concat_axis=0, tiled=True)
-    told = everything[:, size:].reshape(devices, 8, -1).astype(jnp.int32)
-    plan = arrivals(told[:, 0], told[:, 1], me, *front.shape)
+    told = everything[2][..., :2, -NOTED:].reshape(2, 4, 2, 2, 4, 2, NOTED)
+    told = told.transpose(5, 1, 2, 4, 3, 0, 6).reshape(2, devices, NOTED).astype(jnp.int32)
+    plan = arrivals(told[0], told[1], me, *front.shape)
     panel, plan, pattern = lax.optimization_barrier((panel, plan, pattern))
     factor, rounded = cholesky_solve(everything, panel)
     row_side, col_side = spread(rounded)

time: 191 us -> 189 us (0.990)
    pallas_call x1, Pallas kernels: 61.5 us -> 65.2 us  [cholesky_solve(): pl.pallas_call(cholesky_kernel, out_shape=(jax.ShapeDtypeStruct((own, siz...]
    pallas_call x1, Pallas kernels: 63.3 us -> 60.4 us  [spread(): pl.pallas_call(spread_kernel, out_shape=(side, side), in_specs=[pl.BlockS...]
  transfers between devices with their start and end apart: 1 -> 1, of which waited for: 0 -> 0; matrix products, arithmetic and copies ran while one was open for 2% -> 1% of each run, Pallas kernels for 66% -> 67%
where the time goes in v4:
time: 189 us; the launch traced here: 187 us
  Pallas kernels  174 us (92%)
  starting transfers between devices  5.5 us (3%)
  local copies, waits for them, and re-layouts  4.05 us (2%)
  other arithmetic  3.31 us (2%)
    pallas_call x1, Pallas kernels, cholesky_solve(): pl.pallas_call(cholesky_kernel, out_shape=(jax.ShapeDtypeStruct((own, siz...  65.2 us
    pallas_call x1, Pallas kernels, spread(): pl.pallas_call(spread_kernel, out_shape=(side, side), in_specs=[pl.BlockS...  60.4 us
    pallas_call x1, Pallas kernels, gather(): pl.pallas_call(gather_kernel, out_shape=(jax.ShapeDtypeStruct((2, RING, R...  30.2 us
    pallas_call x1, Pallas kernels, finish(): pl.pallas_call(finish_kernel, out_shape=jax.ShapeDtypeStruct(front.shape,...  14 us
    all_to_all x1, starting transfers between devices, per_device(): lax.all_to_all(outgoing, ('row', 'col'), split_axis=0, concat_axis=0, til...  5.5 us
    pallas_call x1, Pallas kernels, pack(): pl.pallas_call(pack_kernel, out_shape=jax.ShapeDtypeStruct((2 * devices,...  3.88 us
  transfers between devices with their start and end apart: 1, of which 0 were waited for; matrix products, arithmetic and copies ran while one was open for 1% of the time, Pallas kernels for 67%

profile of v4, /device:TPU:1, one launch (start us, length us, event | category | flops | bytes accessed | tf_op | source)
XLA Modules:
  0.0 187.3 jit_solution(17679073593636548399)
XLA Ops:
  0.6 0.1 pad.7.clone
  0.7 1.3 add_convert_fusion.notes_ref
  2.0 30.2 %pivot_gather.1 = (f32[2,4,4,4,8,384]{5,4,3,2,1,0:T(8,128)}, f32[2,4,4,4,8,384]{5,4,3,2,1,0:T(8,128)}, f32[2,4,4,4,8,384]{5,4,3,2,1,0:T(8,128)}) custom-call(f32[8,1024]{1,0:T(8,128)} %pivot_ref.1, f32[8,128]{1,0:T(8,128)} %add_convert_fusion.notes_ref), custom_call_target="tpu_custom_call" | custom-call | tf_op jit(solution)/shard_map/pivot_gather/pallas_call | solution.py:198
  32.2 3.9 %pack.1 = bf16[256,128,128]{2,1,0:T(8,128)(2,1)} custom-call(s32[128]{0:T(128)} %bitcast.17, bf16[128,128,128]{2,1,0:T(8,128)(2,1)} %blocks_ref.1), custom_call_target="tpu_custom_call" | custom-call | tf_op jit(solution)/shard_map/pack/pallas_call | solution.py:70
  36.1 0.0 copy-start.1
  36.1 0.0 copy-start.5
  36.1 0.0 copy-start.2
  36.2 5.5 %all-to-all-start = ((bf16[256,128,128]{2,1,0:T(8,128)(2,1)}), bf16[256,128,128]{2,1,0:T(8,128)(2,1)}, u32[]{:S(2)}, u32[]{:S(2)}) async-start(bf16[256,128,128]{2,1,0:T(8,128)(2,1)} %pack.1), calls=%async_computation | async-start | bytes 16777216 | tf_op jit(solution)/shard_map/all_to_all | solution.py:628
  41.7 0.0 copy-done.1
  41.7 0.1 copy.15
  42.0 0.1 select_reduce_fusion.3
  42.1 0.2 select_reduce_fusion.2
  42.3 0.2 convert_reduce_fusion
  42.5 0.1 select_reduce_fusion
  42.6 0.6 add_select_fusion
  43.2 0.7 convert_reduce_fusion.1.start_ref
  43.9 0.0 copy-done.5
  43.9 0.7 copy.13.pattern_ref
  44.6 0.0 copy-done.2
  44.6 0.0 copy-start.3
  44.6 1.4 copy-done.3
  46.0 0.0 copy-start.4
  46.0 1.0 copy-done.4
  47.0 65.2 %cholesky_solve.1 = (f32[128,1024]{1,0:T(8,128)}, bf16[128,1024]{1,0:T(8,128)(2,1)S(1)}) custom-call(f32[2,4,4,4,8,384]{5,4,3,2,1,0:T(8,128)S(1)} %copy-done.2, f32[2,4,4,4,8,384]{5,4,3,2,1,0:T(8,128)S(1)} %copy-done.3, f32[2,4,4,4,8,384]{5,4,3,2,1,0:T(8,128)S(1)} %copy-done.1, f32[128,1024]{1,0:T(8,128)S(1)} %copy-done.4), custom_call_target="tpu_custom_call" | custom-call | flops 10000000000 | bytes 10000000 | tf_op jit(solution)/shard_map/cholesky_solve/pallas_call | solution.py:298
  112.2 0.0 copy-start
  112.2 0.7 copy-done
  112.9 60.4 %factor_spread.1 = (bf16[4,2,2,128,1024]{4,3,2,1,0:T(8,128)(2,1)}, bf16[4,2,2,128,1024]{4,3,2,1,0:T(8,128)(2,1)}) custom-call(bf16[128,1024]{1,0:T(8,128)(2,1)} %copy-done), custom_call_target="tpu_custom_call" | custom-call | tf_op jit(solution)/shard_map/factor_spread/pallas_call | solution.py:469
  173.3 0.0 all-to-all-done.arrived_ref
  173.3 14.0 %finish.1 = f32[2048,1024]{1,0:T(8,128)} custom-call(s32[260]{0:T(512)} %get-tuple-element.22.slot_ref, s32[260]{0:T(512)} %get-tuple-element.23.place_ref, s32[9]{0:T(128)} %convert_reduce_fusion.1.start_ref, s32[16,8]{1,0:T(8,128)} %copy.13.pattern_ref, f32[2048,1024]{1,0:T(8,128)} %front_ref.1, bf16[256,128,128]{2,1,0:T(8,128)(2,1)} %all-to-all-done.arrived_ref, ...), custom_call_target="tpu_custom_call" | custom-call | tf_op jit(solution)/shard_map/finish/pallas_call | solution.py:573
  (9 shorter events, 0.2 us)
Async XLA Ops:
  36.1 5.5 %copy-start.1 = (f32[2,4,4,4,8,384]{5,4,3,2,1,0:T(8,128)S(1)}, f32[2,4,4,4,8,384]{5,4,3,2,1,0:T(8,128)}, u32[]{:S(2)}) copy-start(f32[2,4,4,4,8,384]{5,4,3,2,1,0:T(8,128)} %get-tuple-element.21.right_ref) | copy-start | bytes 4718596
  36.1 7.8 %copy-start.5 = (s32[16,8]{0,1:T(8,128)S(1)}, s32[16,8]{0,1:T(8,128)}, u32[]{:S(2)}) copy-start(s32[16,8]{0,1:T(8,128)} %param.13) | copy-start | bytes 1540
  36.1 8.4 %copy-start.2 = (f32[2,4,4,4,8,384]{5,4,3,2,1,0:T(8,128)S(1)}, f32[2,4,4,4,8,384]{5,4,3,2,1,0:T(8,128)}, u32[]{:S(2)}) copy-start(f32[2,4,4,4,8,384]{5,4,3,2,1,0:T(8,128)} %get-tuple-element.27.left_ref) | copy-start | bytes 4718596
  36.2 137.1 %all-to-all-start = ((bf16[256,128,128]{2,1,0:T(8,128)(2,1)}), bf16[256,128,128]{2,1,0:T(8,128)(2,1)}, u32[]{:S(2)}, u32[]{:S(2)}) async-start(bf16[256,128,128]{2,1,0:T(8,128)(2,1)} %pack.1), calls=%async_computation | async-start | bytes 16777216 | tf_op jit(solution)/shard_map/all_to_all | solution.py:628
  44.6 1.4 copy-start.3
  46.0 1.0 copy-start.4
  112.2 0.7 copy-start
